TPU v7x, 32 devices: a whole 2x2x4 slice. The times are simulated.
32 devices in a mesh: groups: 2 (over x), blk: 16 (over z, y, core).
Axes of the slice: x: 2, y: 2, z: 4, core: 2. Of those that a mesh axis runs over, the one named last changes fastest.
Arguments:
- rows: bfloat16 [131072, 768], P(('groups', 'blk')), parts along dimension 0, may hold values from -8 to 8, as said below
- centroids: bfloat16 [8192, 768], P(('groups', 'blk')), parts along dimension 0, may hold values from -4 to 4, as said below
- lists: int32 [512, 6], P(('groups', 'blk')), parts along dimension 0, may hold values from 0 to 15, as said below
Outputs:
- new_centroids: float32 [8192, 768], P(('groups', 'blk')), parts along dimension 0
- log_totals: float32 [131072], P(('groups', 'blk')), parts along dimension 0
There are 2 independent parts, one for each index of `groups`. A program takes and returns all parts, laid end to end along the dimension named above; each array names one. Nothing has to cross between parts.
Inputs may be any that keep to these rules, and one draw needn't show every extreme that they name: `rows`: embeddings of order one. `centroids`: centroids of order one half. `lists`: the 6 entries of a block are distinct panel numbers. Block b is held by device q = b // 16 along blk; every listed panel lies within cycle distance 6 of panel q (indices taken modulo 16), panel q itself is always listed, and distance 6 is reached. Panels are listed unevenly.
All inputs are finite; a program needn't handle non-finite values.
Results may differ from a plain program's by a relative error of at most 0.00056.
Values may be sent and summed in bfloat16 or wider, within the bound.
No kernel may reach another device: no remote copies, remote signals or barrier semaphores. Data moves between devices by JAX's collectives and lax.ppermute only.
A program may use at most 128 MiB of HBM per device.

v0:
```python
import functools
import math

import jax
import jax.numpy as jnp
from jax import lax
from jax.experimental import pallas as pl
from jax.experimental.pallas import tpu as pltpu
from jax.sharding import PartitionSpec as P

BLOCK = 256
SPAN = 6
LOGIT_SCALE = 0.25
PRIOR_MASS = 8.0
LOG2E = math.log2(math.e)
LINK_SCALE = 1.0 / 16.0
EXTRA = 8
VMEM_GRANT = 42 << 20


def grid_plan():
    return 0, (
        ((1, 0, None), (2, 0, 4)),
        ((6, 0, -4), (3, 2, None)),
        ((5, 3, 4), (7, 6, None)),
    )


def ring_plan():
    reach = (SPAN + 1) // 2
    return reach, tuple(
        ((reach + hop + 1, reach + hop, 2), (reach - hop - 1, reach - hop, -2)) for hop in range(reach)
    )


def plan_of(count):
    return grid_plan() if count == 16 else ring_plan()


def chip_place(panel, device, count):
    if count == 16:
        return (device // 4 - panel // 4) % 4 * 2 + ((panel ^ device) >> 1 & 1)
    return (device // 2 - panel // 2 + (SPAN + 1) // 2) % (count // 2)


def moved(value, shift):
    count = lax.axis_size("blk")
    if shift is None:
        return lax.ppermute(value, "blk", [(i, i ^ 2) for i in range(count)])
    return lax.ppermute(value, "blk", [(i, (i + shift) % count) for i in range(count)])


def other_core(value):
    count = lax.axis_size("blk")
    return lax.ppermute(value, "blk", [(i, i ^ 1) for i in range(count)])


def packed(value):
    return (value * LINK_SCALE).astype(jnp.float16)


def pairs_of(slots, room):
    blocks, listed = slots.shape
    hit = slots[:, :, None] == jnp.arange(room, dtype=jnp.int32)
    listing = jnp.any(hit, axis=1)
    code = 8 * jnp.arange(blocks, dtype=jnp.int32)[:, None] + jnp.sum(
        jnp.where(hit, jnp.arange(listed, dtype=jnp.int32)[None, :, None], 0), axis=1
    )
    before = jnp.arange(blocks)[:, None] > jnp.arange(blocks)[None, :]
    rank = jnp.sum(jnp.where(before[:, :, None] & listing[None], 1, 0), axis=1)
    chosen = listing[:, :, None] & (rank[:, :, None] == jnp.arange(blocks))
    order = jnp.sum(jnp.where(chosen, code[:, :, None], 0), axis=0)
    return order.reshape(-1).astype(jnp.int32), jnp.sum(listing, axis=0).astype(jnp.int32)


def local_slots(members):
    return [2 * q + core for q in members for core in (0, 1)]


def some_pairs(order_ref, counts_ref, slot, blocks, first, number):
    work = []
    for i in range(number):
        code = order_ref[slot * blocks + jnp.minimum(first + i, counts_ref[slot] - 1)]
        work.append((first + i, code >> 3, (code & 7) * blocks + (code >> 3)))
    return work


def by_fours(count, act):
    fours = count // 4
    lax.fori_loop(0, fours, lambda k, _: (act(4 * k, 4), 0)[1], 0)
    lax.fori_loop(2 * fours, (count + 1) // 2, lambda k, _: (act(2 * k, 2), 0)[1], 0)


def by_eights(count, act):
    eights = count // 8
    lax.fori_loop(0, eights, lambda k, _: (act(8 * k, 8), 0)[1], 0)
    fours = (count - 8 * eights) // 4

    @pl.when(fours == 1)
    def _():
        act(8 * eights, 4)

    lax.fori_loop(
        4 * eights + 2 * fours, (count + 1) // 2, lambda k, _: (act(2 * k, 2), 0)[1], 0
    )


def rows_of(x, block):
    return x[pl.ds(pl.multiple_of(block * BLOCK, BLOCK), BLOCK)]


def find_norms(piece_refs, panels, norms):
    for p, piece in enumerate(piece_refs):
        if piece is not None:
            panels[p] = piece[...]
        wide = panels[p].astype(jnp.float32)
        norm = jnp.sum(wide * wide, axis=1, keepdims=True)
        norms[p] = jnp.broadcast_to(norm * (0.5 * LOGIT_SCALE * LOG2E), norms.shape[1:])


def tile_of(panel, norm, block):
    scores = lax.dot_general(
        panel, block, (((1,), (1,)), ((), ())), preferred_element_type=jnp.float32
    )
    scores = scores * (LOGIT_SCALE * LOG2E) - jnp.concatenate([norm, norm], axis=1)
    top = jnp.max(scores, axis=0, keepdims=True)
    powers = jnp.exp2(scores - top)
    return powers, top, jnp.sum(powers, axis=0, keepdims=True)


def score_loop(
    slots, order_ref, counts_ref, x, panels, norms, tops, masses, tiles, here, done
):
    blocks = x.shape[0] // BLOCK
    tops[...] = jnp.full_like(tops, -jnp.inf)
    masses[...] = jnp.zeros_like(masses)
    starts = [jnp.int32(0)]
    for slot in slots:
        starts.append(starts[-1] + counts_ref[slot])
    count = starts.pop()

    def pair(j):
        p = sum([(j >= start).astype(jnp.int32) for start in starts[1:]], jnp.int32(0))
        first, slot = starts[0], jnp.int32(slots[0])
        for later, start in zip(slots[1:], starts[1:]):
            first = jnp.where(j >= start, start, first)
            slot = jnp.where(j >= start, later, slot)
        code = order_ref[slot * blocks + j - first]
        return p, p * blocks + j - first, code >> 3, (code & 7) * blocks + (code >> 3)

    def some(first, number):
        work = [pair(jnp.minimum(first + i, count - 1)) for i in range(number)]
        for _, _, b, _ in work:
            here(b)
        found = [tile_of(panels[p], norms[p], rows_of(x, b)) for p, _, b, _ in work]
        for (_, tile, _, at), (powers, top, mass) in zip(work, found):
            tiles[tile] = powers
            tops[pl.ds(at, 1)] = top
            masses[pl.ds(at, 1)] = mass
        for i, (_, tile, _, _) in enumerate(work):
            if number == 2 and i:
                pl.when(first + i < count)(functools.partial(done, tile))
            else:
                done(tile)

    by_eights(count, some)


def sum_loop(slots, order_ref, counts_ref, x, shares, acc, totals, tiles, ready):
    blocks = x.shape[0] // BLOCK
    cent = totals.shape[1]
    for p, slot in enumerate(slots):

        def some(first, number):
            work = some_pairs(order_ref, counts_ref, slot, blocks, first, number)
            for i, (j, _, _) in enumerate(work):
                if number == 2 and i:
                    pl.when(j < counts_ref[slot])(functools.partial(ready, p, j))
                else:
                    ready(p, j)
            partial, count = None, None
            for i, (j, b, at) in enumerate(work):
                share = shares[pl.ds(at, 1)]
                if number == 2 and i:
                    share = share * (j < counts_ref[slot]).astype(jnp.float32)
                    j = jnp.minimum(j, counts_ref[slot] - 1)
                weights = (tiles[p * blocks + j] * share).astype(jnp.bfloat16)
                wide = weights.astype(jnp.float32)
                wide = wide[:, :128] + wide[:, 128:]
                product = jnp.dot(weights, rows_of(x, b), preferred_element_type=jnp.float32)
                partial = product if partial is None else partial + product
                count = wide if count is None else count + wide
            totals[p] += count
            acc[p][pl.ds(0, cent)] += partial

        by_fours(counts_ref[slot], some)


def clear_sums(acc, totals):
    for ref in acc:
        ref[...] = jnp.zeros_like(ref)
    totals[...] = jnp.zeros_like(totals)


def store_totals(acc, totals):
    cent = totals.shape[1]
    for p, ref in enumerate(acc):
        row = jnp.sum(totals[p].T, axis=0, keepdims=True)
        ref[pl.ds(cent, EXTRA), pl.ds(0, cent)] = jnp.broadcast_to(row, (EXTRA, cent))


def over_tiles(slots, counts_ref, act):
    for p, slot in enumerate(slots):
        lax.fori_loop(0, counts_ref[slot], lambda i, _, p=p: (act(p, i), 0)[1], 0)


def score_kernel(slots, fetch, order_ref, counts_ref, rows_ref, *refs):
    pieces = len(slots)
    piece_refs = refs[:pieces]
    tiles_ref, tops, masses = refs[pieces : pieces + 3]
    refs = refs[pieces + 3 :]
    x = refs[0] if fetch else rows_ref
    panels, norms, tiles, tile_sem = refs[1:5] if fetch else refs[:4]
    blocks = x.shape[0] // BLOCK
    here = lambda b: None
    if fetch:
        row_sem, fetched, panel_sem = refs[5:]
        brought = [
            pltpu.make_async_copy(ref, panels.at[p], panel_sem.at[p])
            for p, ref in enumerate(piece_refs)
        ]
        for copy in brought:
            copy.start()

        def bring(b):
            span = pl.ds(pl.multiple_of(b * BLOCK, BLOCK), BLOCK)
            return pltpu.make_async_copy(rows_ref.at[span], x.at[span], row_sem.at[b])

        for b in range(blocks):
            bring(b).start()
        fetched[0] = 0

        def here(b):
            first = fetched[0]
            lax.fori_loop(first, b + 1, lambda k, _: (bring(k).wait(), 0)[1], 0)
            fetched[0] = jnp.maximum(first, b + 1)

        for copy in brought:
            copy.wait()
        piece_refs = [None] * pieces

    find_norms(piece_refs, panels, norms)

    def outgoing(j):
        return pltpu.make_async_copy(tiles.at[j], tiles_ref.at[j], tile_sem.at[j])

    score_loop(
        slots, order_ref, counts_ref, x, panels, norms, tops, masses, tiles, here,
        lambda j: outgoing(j).start(),
    )
    here(blocks - 1)
    over_tiles(slots, counts_ref, lambda p, i: outgoing(p * blocks + i).wait())


def sum_kernel(slots, sources, order_ref, counts_ref, x, shares, *refs):
    pieces = len(slots)
    arrays = len({which for which, _ in sources})
    tiles_refs, refs = refs[:arrays], refs[arrays:]
    out_refs = refs[:pieces]
    blocks = x.shape[0] // BLOCK
    totals, tiles, tile_sem = refs[pieces:]

    def incoming(p, i):
        which, first = sources[p]
        j = p * blocks + i
        return pltpu.make_async_copy(tiles_refs[which].at[first + i], tiles.at[j], tile_sem.at[j])

    over_tiles(slots, counts_ref, lambda p, i: incoming(p, i).start())
    clear_sums(out_refs, totals)
    sum_loop(
        slots, order_ref, counts_ref, x, shares, out_refs, totals, tiles,
        lambda p, i: incoming(p, i).wait(),
    )
    store_totals(out_refs, totals)


def middle_kernel(slots, listed, earlier, order_ref, counts_ref, x, *refs):
    pieces = len(slots)
    stat_refs = refs[: 2 * earlier]
    piece_refs = refs[2 * earlier : 2 * earlier + pieces]
    refs = refs[2 * earlier + pieces :]
    logs_ref, shares = refs[:2]
    out_refs = refs[2 : 2 + pieces]
    panels, norms, tiles, tops, masses, totals = refs[2 + pieces :]
    blocks = x.shape[0] // BLOCK
    clear_sums(out_refs, totals)
    find_norms(piece_refs, panels, norms)
    score_loop(
        slots, order_ref, counts_ref, x, panels, norms, tops, masses, tiles,
        lambda b: None, lambda j: None,
    )
    width = tops.shape[1]
    top = functools.reduce(jnp.maximum, [ref[...] for ref in stat_refs[:earlier]], tops[...])
    mass = functools.reduce(jnp.add, [ref[...] for ref in stat_refs[earlier:]], masses[...])
    top = top.reshape(listed, blocks, width)
    mass = mass.reshape(listed, blocks, width)
    highest = jnp.max(top, axis=0)
    factor = jnp.exp2(top - highest[None])
    whole = jnp.sum(factor * mass, axis=0)
    logs_ref[...] = (highest + jnp.log2(whole)) * (1.0 / LOG2E)
    shares[...] = (factor / whole[None]).reshape(listed * blocks, width)
    sum_loop(slots, order_ref, counts_ref, x, shares, out_refs, totals, tiles, lambda p, i: None)
    store_totals(out_refs, totals)


SMEM = pl.BlockSpec(memory_space=pltpu.SMEM)
HBM = pl.BlockSpec(memory_space=pltpu.HBM)
VMEM = pl.BlockSpec(memory_space=pltpu.VMEM)


class Sizes:
    def __init__(self, rows, blocks, listed, cent):
        self.blocks, self.listed, self.cent = blocks, listed, cent
        self.width = rows.shape[1]
        self.stats = jax.ShapeDtypeStruct((listed * blocks, BLOCK), jnp.float32)
        self.sums = jax.ShapeDtypeStruct((cent + EXTRA, self.width), jnp.float32)
        self.tiles = jax.ShapeDtypeStruct((5 * blocks, cent, BLOCK), jnp.float32)

    def cost(self, slots, products):
        pairs = self.blocks * self.listed * len(slots) / 14
        return pl.CostEstimate(
            flops=int(2 * products * pairs * self.cent * BLOCK * self.width),
            bytes_accessed=int(2 * self.blocks * BLOCK * self.width + 4 * pairs * self.cent * BLOCK),
            transcendentals=int(pairs * self.cent * BLOCK),
        )

    def panels(self, pieces):
        return pltpu.VMEM((pieces, self.cent, self.width), jnp.bfloat16)

    def columns(self, pieces):
        return pltpu.VMEM((pieces, self.cent, 128), jnp.float32)

    def tile_scratch(self, pieces):
        return pltpu.VMEM((pieces * self.blocks, self.cent, BLOCK), jnp.float32)


def score_group(sizes, slots, order, counts, rows, pieces, fetch):
    count = len(pieces)
    outs = (sizes.tiles, sizes.stats, sizes.stats)
    rows_outs, rows_scratch = (), []
    if fetch:
        rows_outs = (jax.ShapeDtypeStruct(rows.shape, rows.dtype),)
        rows_scratch = [
            pltpu.SemaphoreType.DMA((sizes.blocks,)),
            pltpu.SMEM((1,), jnp.int32),
            pltpu.SemaphoreType.DMA((count,)),
        ]
    return pl.pallas_call(
        functools.partial(score_kernel, slots, fetch),
        out_shape=outs + rows_outs,
        in_specs=[SMEM, SMEM] + ([HBM] * (1 + count) if fetch else [VMEM] * (1 + count)),
        out_specs=(HBM, VMEM, VMEM) + (VMEM,) * len(rows_outs),
        scratch_shapes=[
            sizes.panels(count),
            sizes.columns(count),
            sizes.tile_scratch(count),
            pltpu.SemaphoreType.DMA((count * sizes.blocks,)),
        ]
        + rows_scratch,
        compiler_params=pltpu.CompilerParams(vmem_limit_bytes=VMEM_GRANT),
        cost_estimate=sizes.cost(slots, 1),
        name="score_group",
    )(order, counts, rows, *pieces)


def sum_group(sizes, slots, order, counts, rows, shares, places, tiles):
    count = len(slots)
    used = sorted({places[slot][0] for slot in slots})
    sources = [(used.index(places[slot][0]), places[slot][1]) for slot in slots]
    return pl.pallas_call(
        functools.partial(sum_kernel, slots, sources),
        out_shape=(sizes.sums,) * count,
        in_specs=[SMEM, SMEM, VMEM, VMEM] + [HBM] * len(used),
        out_specs=(VMEM,) * count,
        scratch_shapes=[
            sizes.columns(count),
            sizes.tile_scratch(count),
            pltpu.SemaphoreType.DMA((count * sizes.blocks,)),
        ],
        compiler_params=pltpu.CompilerParams(vmem_limit_bytes=VMEM_GRANT),
        cost_estimate=sizes.cost(slots, 1),
        name="sum_group",
    )(order, counts, rows, shares, *[tiles[which] for which in used])


def middle_group(sizes, slots, order, counts, rows, tops, masses, pieces):
    count = len(pieces)
    earlier = len(tops)
    return pl.pallas_call(
        functools.partial(middle_kernel, slots, sizes.listed, earlier),
        out_shape=(jax.ShapeDtypeStruct((sizes.blocks, BLOCK), jnp.float32), sizes.stats)
        + (sizes.sums,) * count,
        in_specs=[SMEM, SMEM, VMEM] + [VMEM] * (2 * earlier + count),
        out_specs=(VMEM, VMEM) + (VMEM,) * count,
        scratch_shapes=[
            sizes.panels(count),
            sizes.columns(count),
            sizes.tile_scratch(count),
            pltpu.VMEM(sizes.stats.shape, jnp.float32),
            pltpu.VMEM(sizes.stats.shape, jnp.float32),
            sizes.columns(count),
        ],
        compiler_params=pltpu.CompilerParams(vmem_limit_bytes=VMEM_GRANT),
        cost_estimate=sizes.cost(slots, 2),
        name="middle_group",
    )(order, counts, rows, *tops, *masses, *pieces)


def add_kernel(mine_ref, back_ref, out_ref):
    out_ref[...] = mine_ref[...] * LINK_SCALE + back_ref[...]


def scaled_sum(mine, back):
    return pl.pallas_call(
        add_kernel,
        out_shape=jax.ShapeDtypeStruct(mine.shape, mine.dtype),
        in_specs=[VMEM, VMEM],
        out_specs=VMEM,
        compiler_params=pltpu.CompilerParams(vmem_limit_bytes=VMEM_GRANT),
        cost_estimate=pl.CostEstimate(flops=30 * 10**9, bytes_accessed=12 * mine.size, transcendentals=0),
        name="scaled_sum",
    )(mine, back)


def on_device(rows, centroids, lists):
    count = lax.axis_size("blk")
    device = lax.axis_index("blk")
    cent = centroids.shape[0]
    own, stages = plan_of(count)
    groups = [(own,)] + [tuple(q for q, _, _ in stage) for stage in stages]
    slots = (2 * chip_place(lists, device, count) + ((lists ^ device) & 1)).astype(jnp.int32)
    sizes = Sizes(rows, *slots.shape, cent)
    order, counts = pairs_of(slots, 2 * max(q for members in groups for q in members) + 2)

    near, far = {own: centroids}, {}
    tiles, tops, masses, places = [], [], [], {}

    def score(slots, fetch=False):
        pieces = [(far if slot & 1 else near)[slot >> 1] for slot in slots]
        for p, slot in enumerate(slots):
            places[slot] = (len(tiles), p * sizes.blocks)
        return score_group(sizes, slots, order, counts, rows, pieces, fetch)

    for number, stage in enumerate(stages):
        arriving = [moved(near[source], shift) for _, source, shift in stage]
        for q in groups[number]:
            far[q] = other_core(near[q])
        if number == 0:
            scored = score([2 * own], fetch=True)
        elif number == 1:
            scored = score([2 * own + 1] + local_slots(groups[1]))
        else:
            scored = score(local_slots(groups[number]))
        arriving, scored, near, far = lax.optimization_barrier((arriving, scored, near, far))
        if number == 0:
            rows = scored[3]
        tiles.append(scored[0])
        tops.append(scored[1])
        masses.append(scored[2])
        for (q, _, _), value in zip(stage, arriving):
            near[q] = value
    last = groups[-1]
    near_slots, far_slots = [2 * q for q in last], [2 * q + 1 for q in last]
    for q in last:
        far[q] = other_core(near[q])
    scored = score(near_slots)
    tiles.append(scored[0])
    tops.append(scored[1])
    masses.append(scored[2])
    log_totals, shares, *far_sums = middle_group(
        sizes, far_slots, order, counts, rows, tops, masses, [far[q] for q in last]
    )
    near_sums = sum_group(sizes, near_slots, order, counts, rows, shares, places, tiles)
    mine = dict(zip(last, near_sums))
    crossed = {q: other_core(packed(v)) for q, v in zip(last, far_sums)}
    total = {q: mine[q] * LINK_SCALE + crossed[q].astype(jnp.float32) for q in last}

    back = {q: [] for members in groups for q in members}
    for members, stage in zip(reversed(groups[:-1]), reversed(stages)):
        stage = sorted(stage, key=lambda move: move[2] is None)
        leaving = [total[q].astype(jnp.float16) for q, _, _ in stage]
        leaving, shares = lax.optimization_barrier((leaving, shares))
        arriving = [
            moved(value, shift if shift is None else -shift)
            for value, (_, _, shift) in zip(leaving, stage)
        ]
        sums = sum_group(sizes, local_slots(members), order, counts, rows, shares, places, tiles)
        crossed = {q: other_core(packed(v)) for q, v in zip(members, sums[1::2])}
        arriving = lax.optimization_barrier(arriving)
        for value, (_, source, _) in zip(arriving, stage):
            back[source].append(value.astype(jnp.float32))
        for q, near_sum in zip(members, sums[::2]):
            if back[q]:
                part = scaled_sum(near_sum, functools.reduce(jnp.add, back[q]))
            else:
                part = near_sum * LINK_SCALE
            total[q] = part + crossed[q].astype(jnp.float32)
    own_sums = total[own] * (1.0 / LINK_SCALE)
    updated = (own_sums[:cent] + PRIOR_MASS * centroids.astype(jnp.float32)) / (
        own_sums[cent, :cent][:, None] + PRIOR_MASS
    )
    return updated, log_totals.reshape(-1)


def solution(mesh):
    placed = P(("groups", "blk"), None)
    return jax.shard_map(
        on_device,
        mesh=mesh,
        in_specs=(placed, placed, placed),
        out_specs=(placed, P(("groups", "blk"))),
        check_vma=False,
    )
```

profile of v0, /device:TPU:2, one launch (start us, length us, event | category | flops | bytes accessed | tf_op | source)
XLA Modules:
  0.0 107.8 jit_solution(13130271943533764904)
XLA Ops:
  0.6 1.6 %collective-permute-start = (bf16[256,768]{1,0:T(8,128)(2,1)}, bf16[256,768]{1,0:T(8,128)(2,1)S(1)}, u32[]{:S(2)}, u32[]{:S(2)}) collective-permute-start(bf16[256,768]{1,0:T(8,128)(2,1)} %refs_0_.1), channel_id=1, source_target_pairs={{0,2},{1,3},{2,0},{3,1},{4,6},{5,7},{6,4},{7,5},{8,10},{9,11},{10,... | collective-permute-start | bytes 1179656 | tf_op jit(solution)/shard_map/ppermute | solution.py:49
  2.2 1.6 %collective-permute-start.1 = (bf16[256,768]{1,0:T(8,128)(2,1)}, bf16[256,768]{1,0:T(8,128)(2,1)S(1)}, u32[]{:S(2)}, u32[]{:S(2)}) collective-permute-start(bf16[256,768]{1,0:T(8,128)(2,1)} %refs_0_.1), channel_id=1, source_target_pairs={{0,4},{1,5},{2,6},{3,7},{4,8},{5,9},{6,10},{7,11},{8,12},{9,13},{1... | collective-permute-start | bytes 1179656 | tf_op jit(solution)/shard_map/ppermute | solution.py:50
  3.8 0.7 fusion.9
  5.2 1.0 copy-done
  6.2 6.5 %score_group.4 = (f32[80,256,256]{2,1,0:T(8,128)}, f32[96,256]{1,0:T(8,128)S(1)}, f32[96,256]{1,0:T(8,128)S(1)}, bf16[4096,768]{1,0:T(8,128)(2,1)S(1)}) custom-call(s32[256]{0:T(256)S(1)} %reshape.57.order_ref, s32[16]{0:T(128)S(1)} %convert_reduce_fusion.counts_ref, bf16[4096,768]{1,0:T(8,128)(2,1)} %rows_ref.1, bf16[256,768]{1,0:T(8,128)(2,1)S(1)} %copy-done), custom_call_target="tpu_custom_call" | custom-call | flops 690262592 | bytes 8089014 | tf_op jit(solution)/shard_map/score_group/pallas_call | solution.py:358
  12.7 2.2 %collective-permute-done.1.refs_3_ = bf16[256,768]{1,0:T(8,128)(2,1)S(1)} collective-permute-done((bf16[256,768]{1,0:T(8,128)(2,1)}, bf16[256,768]{1,0:T(8,128)(2,1)S(1)}, u32[]{:S(2)}, u32[]{:S(2)}) %collective-permute-start.1) | collective-permute-done | bytes 393248 | tf_op jit(solution)/shard_map/ppermute | solution.py:50
  15.4 1.7 %collective-permute-start.3 = (bf16[256,768]{1,0:T(8,128)(2,1)S(1)}, bf16[256,768]{1,0:T(8,128)(2,1)S(1)}, u32[]{:S(2)}, u32[]{:S(2)}) collective-permute-start(bf16[256,768]{1,0:T(8,128)(2,1)S(1)} %copy-done), channel_id=1, source_target_pairs={{0,12},{1,13},{2,14},{3,15},{4,0},{5,1},{6,2},{7,3},{8,4},{9,5},{1... | collective-permute-start | bytes 1179656 | tf_op jit(solution)/shard_map/ppermute | solution.py:50
  17.6 4.3 %score_group.5 = (f32[80,256,256]{2,1,0:T(8,128)}, f32[96,256]{1,0:T(8,128)S(1)}, f32[96,256]{1,0:T(8,128)S(1)}) custom-call(s32[256]{0:T(256)S(1)} %reshape.57.order_ref, s32[16]{0:T(128)S(1)} %convert_reduce_fusion.counts_ref, bf16[4096,768]{1,0:T(8,128)(2,1)S(1)} %get-tuple-element.68.rows_ref.x, bf16[256,768]{1,0:T(8,128)(2,1)S(1)} %collective-permute-done.2.refs_0_, ...), custom_call_target="tpu_custom_call" | custom-call | flops 3451312896 | bytes 15279250 | tf_op jit(solution)/shard_map/score_group/pallas_call | solution.py:358
  21.9 4.5 %collective-permute-done.3.refs_0_ = bf16[256,768]{1,0:T(8,128)(2,1)S(1)} collective-permute-done((bf16[256,768]{1,0:T(8,128)(2,1)S(1)}, bf16[256,768]{1,0:T(8,128)(2,1)S(1)}, u32[]{:S(2)}, u32[]{:S(2)}) %collective-permute-start.3) | collective-permute-done | bytes 393248 | tf_op jit(solution)/shard_map/ppermute | solution.py:50
  26.4 1.4 %collective-permute-done.4.refs_2_ = bf16[256,768]{1,0:T(8,128)(2,1)S(1)} collective-permute-done((bf16[256,768]{1,0:T(8,128)(2,1)S(1)}, bf16[256,768]{1,0:T(8,128)(2,1)S(1)}, u32[]{:S(2)}, u32[]{:S(2)}) %collective-permute-start.4) | collective-permute-done | bytes 393248 | tf_op jit(solution)/shard_map/ppermute | solution.py:49
  29.6 0.6 collective-permute-done.10.refs_3_
  30.1 9.2 %score_group.6 = (f32[80,256,256]{2,1,0:T(8,128)}, f32[96,256]{1,0:T(8,128)S(1)}, f32[96,256]{1,0:T(8,128)S(1)}) custom-call(s32[256]{0:T(256)S(1)} %reshape.57.order_ref, s32[16]{0:T(128)S(1)} %convert_reduce_fusion.counts_ref, bf16[4096,768]{1,0:T(8,128)(2,1)S(1)} %get-tuple-element.68.rows_ref.x, bf16[256,768]{1,0:T(8,128)(2,1)S(1)} %collective-permute-done.3.refs_0_, ...), custom_call_target="tpu_custom_call" | custom-call | flops 2761050368 | bytes 13481691 | tf_op jit(solution)/shard_map/score_group/pallas_call | solution.py:358
  39.3 1.8 %collective-permute-done.7.refs_0_ = bf16[256,768]{1,0:T(8,128)(2,1)S(1)} collective-permute-done((bf16[256,768]{1,0:T(8,128)(2,1)S(1)}, bf16[256,768]{1,0:T(8,128)(2,1)S(1)}, u32[]{:S(2)}, u32[]{:S(2)}) %collective-permute-start.7) | collective-permute-done | bytes 393248 | tf_op jit(solution)/shard_map/ppermute | solution.py:50
  41.7 4.0 %score_group.7 = (f32[80,256,256]{2,1,0:T(8,128)}, f32[96,256]{1,0:T(8,128)S(1)}, f32[96,256]{1,0:T(8,128)S(1)}) custom-call(s32[256]{0:T(256)S(1)} %reshape.57.order_ref, s32[16]{0:T(128)S(1)} %convert_reduce_fusion.counts_ref, bf16[4096,768]{1,0:T(8,128)(2,1)S(1)} %get-tuple-element.68.rows_ref.x, bf16[256,768]{1,0:T(8,128)(2,1)S(1)} %collective-permute-done.7.refs_0_, ...), custom_call_target="tpu_custom_call" | custom-call | flops 1380525184 | bytes 9886573 | tf_op jit(solution)/shard_map/score_group/pallas_call | solution.py:358
  45.7 6.3 %middle_group.1 = (f32[16,256]{1,0:T(8,128)S(1)}, f32[96,256]{1,0:T(8,128)S(1)}, f32[264,768]{1,0:T(8,128)S(1)}, f32[264,768]{1,0:T(8,128)S(1)}) custom-call(s32[256]{0:T(256)S(1)} %reshape.57.order_ref, s32[16]{0:T(128)S(1)} %convert_reduce_fusion.counts_ref, bf16[4096,768]{1,0:T(8,128)(2,1)S(1)} %get-tuple-element.68.rows_ref.x, ...), custom_call_target="tpu_custom_call" | custom-call | flops 2761050368 | bytes 9886573 | tf_op jit(solution)/shard_map/middle_group/pallas_call | solution.py:399
  52.3 0.6 collective-permute-start.14
  52.8 4.1 %sum_group.4 = (f32[264,768]{1,0:T(8,128)S(1)}, f32[264,768]{1,0:T(8,128)S(1)}) custom-call(s32[256]{0:T(256)S(1)} %reshape.57.order_ref, s32[16]{0:T(128)S(1)} %convert_reduce_fusion.counts_ref, bf16[4096,768]{1,0:T(8,128)(2,1)S(1)} %get-tuple-element.68.rows_ref.x, f32[96,256]{1,0:T(8,128)S(1)} %get-tuple-element.116.shares, ...), custom_call_target="tpu_custom_call" | custom-call | flops 1380525184 | bytes 9886573 | tf_op jit(solution)/shard_map/sum_group/pallas_call | solution.py:380
  57.2 10.6 %collective-permute-start.16 = (f16[264,768]{1,0:T(8,128)(2,1)S(1)}, f16[264,768]{1,0:T(8,128)(2,1)S(1)}, u32[]{:S(2)}, u32[]{:S(2)}) collective-permute-start(f16[264,768]{1,0:T(8,128)(2,1)S(1)} %add_convert_fusion.4), channel_id=1, source_target_pairs={{0,2},{1,3},{2,0},{3,1},{4,6},{5,7},{6,4},{7,5},{8,10},{9,11},{10,... | collective-permute-start | bytes 1216520 | tf_op jit(solution)/shard_map/ppermute | solution.py:49
  67.8 9.5 %sum_group.5 = (f32[264,768]{1,0:T(8,128)S(1)}, f32[264,768]{1,0:T(8,128)S(1)}, f32[264,768]{1,0:T(8,128)S(1)}, f32[264,768]{1,0:T(8,128)S(1)}) custom-call(s32[256]{0:T(256)S(1)} %reshape.57.order_ref, s32[16]{0:T(128)S(1)} %convert_reduce_fusion.counts_ref, bf16[4096,768]{1,0:T(8,128)(2,1)S(1)} %get-tuple-element.68.rows_ref.x, ...), custom_call_target="tpu_custom_call" | custom-call | flops 2761050368 | bytes 13481691 | tf_op jit(solution)/shard_map/sum_group/pallas_call | solution.py:380
  77.5 0.6 collective-permute-start.18
  78.4 0.7 collective-permute-done.17
  80.2 4.2 %sum_group.6 = (f32[264,768]{1,0:T(8,128)S(1)}, f32[264,768]{1,0:T(8,128)S(1)}, f32[264,768]{1,0:T(8,128)S(1)}, f32[264,768]{1,0:T(8,128)S(1)}) custom-call(s32[256]{0:T(256)S(1)} %reshape.57.order_ref, s32[16]{0:T(128)S(1)} %convert_reduce_fusion.counts_ref, bf16[4096,768]{1,0:T(8,128)(2,1)S(1)} %get-tuple-element.68.rows_ref.x, ...), custom_call_target="tpu_custom_call" | custom-call | flops 2761050368 | bytes 13481691 | tf_op jit(solution)/shard_map/sum_group/pallas_call | solution.py:380
  84.7 0.6 collective-permute-start.22
  85.2 8.1 %collective-permute-done.19 = f16[264,768]{1,0:T(8,128)(2,1)S(1)} collective-permute-done((f16[264,768]{1,0:T(8,128)(2,1)S(1)}, f16[264,768]{1,0:T(8,128)(2,1)S(1)}, u32[]{:S(2)}, u32[]{:S(2)}) %collective-permute-start.19) | collective-permute-done | bytes 405536 | tf_op jit(solution)/shard_map/ppermute | solution.py:50
  93.8 1.8 %collective-permute-start.23 = (f16[264,768]{1,0:T(8,128)(2,1)S(1)}, f16[264,768]{1,0:T(8,128)(2,1)S(1)}, u32[]{:S(2)}, u32[]{:S(2)}) collective-permute-start(f16[264,768]{1,0:T(8,128)(2,1)S(1)} %add_convert_fusion.1), channel_id=1, source_target_pairs={{0,12},{1,13},{2,14},{3,15},{4,0},{5,1},{6,2},{7,3},{8,4},{9,5},{1... | collective-permute-start | bytes 1216520 | tf_op jit(solution)/shard_map/ppermute | solution.py:50
  95.9 0.6 copy.6
  96.5 4.7 %sum_group.7 = (f32[264,768]{1,0:T(8,128)S(1)}, f32[264,768]{1,0:T(8,128)S(1)}) custom-call(s32[256]{0:T(256)S(1)} %reshape.57.order_ref, s32[16]{0:T(128)S(1)} %convert_reduce_fusion.counts_ref, bf16[4096,768]{1,0:T(8,128)(2,1)S(1)} %get-tuple-element.68.rows_ref.x, f32[96,256]{1,0:T(8,128)S(1)} %get-tuple-element.116.shares, ...), custom_call_target="tpu_custom_call" | custom-call | flops 1380525184 | bytes 9886573 | tf_op jit(solution)/shard_map/sum_group/pallas_call | solution.py:380
  101.4 1.4 %collective-permute-start.25 = (f16[264,768]{1,0:T(8,128)(2,1)S(1)}, f16[264,768]{1,0:T(8,128)(2,1)S(1)}, u32[]{:S(2)}, u32[]{:S(2)}) collective-permute-start(f16[264,768]{1,0:T(8,128)(2,1)S(1)} %multiply_convert_fusion), channel_id=1, source_target_pairs={{0,1},{1,0},{2,3},{3,2},{4,5},{5,4},{6,7},{7,6},{8,9},{9,8},{10,11... | collective-permute-start | bytes 1216520 | tf_op jit(solution)/shard_map/ppermute | solution.py:55
  102.7 1.8 %collective-permute-done.23 = f16[264,768]{1,0:T(8,128)(2,1)S(1)} collective-permute-done((f16[264,768]{1,0:T(8,128)(2,1)S(1)}, f16[264,768]{1,0:T(8,128)(2,1)S(1)}, u32[]{:S(2)}, u32[]{:S(2)}) %collective-permute-start.23) | collective-permute-done | bytes 405536 | tf_op jit(solution)/shard_map/ppermute | solution.py:50
  104.5 1.1 %collective-permute-done.24 = f16[264,768]{1,0:T(8,128)(2,1)S(1)} collective-permute-done((f16[264,768]{1,0:T(8,128)(2,1)S(1)}, f16[264,768]{1,0:T(8,128)(2,1)S(1)}, u32[]{:S(2)}, u32[]{:S(2)}) %collective-permute-start.24) | collective-permute-done | bytes 405536 | tf_op jit(solution)/shard_map/ppermute | solution.py:49
  106.0 0.8 copy-done.1
  106.8 1.0 fusion
  (68 shorter events, 7.4 us)
Async XLA Ops:
  0.6 12.1 %collective-permute-start = (bf16[256,768]{1,0:T(8,128)(2,1)}, bf16[256,768]{1,0:T(8,128)(2,1)S(1)}, u32[]{:S(2)}, u32[]{:S(2)}) collective-permute-start(bf16[256,768]{1,0:T(8,128)(2,1)} %refs_0_.1), channel_id=1, source_target_pairs={{0,2},{1,3},{2,0},{3,1},{4,6},{5,7},{6,4},{7,5},{8,10},{9,11},{10,... | collective-permute-start | bytes 1179656 | tf_op jit(solution)/shard_map/ppermute | solution.py:49
  2.2 12.7 %collective-permute-start.1 = (bf16[256,768]{1,0:T(8,128)(2,1)}, bf16[256,768]{1,0:T(8,128)(2,1)S(1)}, u32[]{:S(2)}, u32[]{:S(2)}) collective-permute-start(bf16[256,768]{1,0:T(8,128)(2,1)} %refs_0_.1), channel_id=1, source_target_pairs={{0,4},{1,5},{2,6},{3,7},{4,8},{5,9},{6,10},{7,11},{8,12},{9,13},{1... | collective-permute-start | bytes 1179656 | tf_op jit(solution)/shard_map/ppermute | solution.py:50
  3.8 11.1 %collective-permute-start.2 = (bf16[256,768]{1,0:T(8,128)(2,1)}, bf16[256,768]{1,0:T(8,128)(2,1)S(1)}, u32[]{:S(2)}, u32[]{:S(2)}) collective-permute-start(bf16[256,768]{1,0:T(8,128)(2,1)} %refs_0_.1), channel_id=1, source_target_pairs={{0,1},{1,0},{2,3},{3,2},{4,5},{5,4},{6,7},{7,6},{8,9},{9,8},{10,11... | collective-permute-start | bytes 1179656 | tf_op jit(solution)/shard_map/ppermute | solution.py:55
  5.2 1.0 copy-start
  14.9 2.7 %collective-permute-start.5 = (bf16[256,768]{1,0:T(8,128)(2,1)S(1)}, bf16[256,768]{1,0:T(8,128)(2,1)S(1)}, u32[]{:S(2)}, u32[]{:S(2)}) collective-permute-start(bf16[256,768]{1,0:T(8,128)(2,1)S(1)} %collective-permute-done.refs_1_), channel_id=1, source_target_pairs={{0,1},{1,0},{2,3},{3,2},{4,5},{5,4},{6,7},{7,6},{8,9},{9,8},{10,11... | collective-permute-start | bytes 1179656 | tf_op jit(solution)/shard_map/ppermute | solution.py:55
  14.9 2.7 %collective-permute-start.6 = (bf16[256,768]{1,0:T(8,128)(2,1)S(1)}, bf16[256,768]{1,0:T(8,128)(2,1)S(1)}, u32[]{:S(2)}, u32[]{:S(2)}) collective-permute-start(bf16[256,768]{1,0:T(8,128)(2,1)S(1)} %collective-permute-done.1.refs_3_), channel_id=1, source_target_pairs={{0,1},{1,0},{2,3},{3,2},{4,5},{5,4},{6,7},{7,6},{8,9},{9,8},{10,11... | collective-permute-start | bytes 1179656 | tf_op jit(solution)/shard_map/ppermute | solution.py:55
  15.4 11.0 %collective-permute-start.3 = (bf16[256,768]{1,0:T(8,128)(2,1)S(1)}, bf16[256,768]{1,0:T(8,128)(2,1)S(1)}, u32[]{:S(2)}, u32[]{:S(2)}) collective-permute-start(bf16[256,768]{1,0:T(8,128)(2,1)S(1)} %copy-done), channel_id=1, source_target_pairs={{0,12},{1,13},{2,14},{3,15},{4,0},{5,1},{6,2},{7,3},{8,4},{9,5},{1... | collective-permute-start | bytes 1179656 | tf_op jit(solution)/shard_map/ppermute | solution.py:50
  17.1 10.7 %collective-permute-start.4 = (bf16[256,768]{1,0:T(8,128)(2,1)S(1)}, bf16[256,768]{1,0:T(8,128)(2,1)S(1)}, u32[]{:S(2)}, u32[]{:S(2)}) collective-permute-start(bf16[256,768]{1,0:T(8,128)(2,1)S(1)} %collective-permute-done.1.refs_3_), channel_id=1, source_target_pairs={{0,2},{1,3},{2,0},{3,1},{4,6},{5,7},{6,4},{7,5},{8,10},{9,11},{10,... | collective-permute-start | bytes 1179656 | tf_op jit(solution)/shard_map/ppermute | solution.py:49
  27.9 1.7 %collective-permute-start.9 = (bf16[256,768]{1,0:T(8,128)(2,1)S(1)}, bf16[256,768]{1,0:T(8,128)(2,1)S(1)}, u32[]{:S(2)}, u32[]{:S(2)}) collective-permute-start(bf16[256,768]{1,0:T(8,128)(2,1)S(1)} %collective-permute-done.3.refs_0_), channel_id=1, source_target_pairs={{0,1},{1,0},{2,3},{3,2},{4,5},{5,4},{6,7},{7,6},{8,9},{9,8},{10,11... | collective-permute-start | bytes 1179656 | tf_op jit(solution)/shard_map/ppermute | solution.py:55
  27.9 2.3 %collective-permute-start.10 = (bf16[256,768]{1,0:T(8,128)(2,1)S(1)}, bf16[256,768]{1,0:T(8,128)(2,1)S(1)}, u32[]{:S(2)}, u32[]{:S(2)}) collective-permute-start(bf16[256,768]{1,0:T(8,128)(2,1)S(1)} %collective-permute-done.4.refs_2_), channel_id=1, source_target_pairs={{0,1},{1,0},{2,3},{3,2},{4,5},{5,4},{6,7},{7,6},{8,9},{9,8},{10,11... | collective-permute-start | bytes 1179656 | tf_op jit(solution)/shard_map/ppermute | solution.py:55
  28.4 12.8 %collective-permute-start.7 = (bf16[256,768]{1,0:T(8,128)(2,1)S(1)}, bf16[256,768]{1,0:T(8,128)(2,1)S(1)}, u32[]{:S(2)}, u32[]{:S(2)}) collective-permute-start(bf16[256,768]{1,0:T(8,128)(2,1)S(1)} %collective-permute-done.4.refs_2_), channel_id=1, source_target_pairs={{0,4},{1,5},{2,6},{3,7},{4,8},{5,9},{6,10},{7,11},{8,12},{9,13},{1... | collective-permute-start | bytes 1179656 | tf_op jit(solution)/shard_map/ppermute | solution.py:50
  28.7 12.5 %collective-permute-start.8 = (bf16[256,768]{1,0:T(8,128)(2,1)S(1)}, bf16[256,768]{1,0:T(8,128)(2,1)S(1)}, u32[]{:S(2)}, u32[]{:S(2)}) collective-permute-start(bf16[256,768]{1,0:T(8,128)(2,1)S(1)} %collective-permute-done.3.refs_0_), channel_id=1, source_target_pairs={{0,2},{1,3},{2,0},{3,1},{4,6},{5,7},{6,4},{7,5},{8,10},{9,11},{10,... | collective-permute-start | bytes 1179656 | tf_op jit(solution)/shard_map/ppermute | solution.py:49
  41.2 4.5 %collective-permute-start.11 = (bf16[256,768]{1,0:T(8,128)(2,1)S(1)}, bf16[256,768]{1,0:T(8,128)(2,1)S(1)}, u32[]{:S(2)}, u32[]{:S(2)}) collective-permute-start(bf16[256,768]{1,0:T(8,128)(2,1)S(1)} %collective-permute-done.7.refs_0_), channel_id=1, source_target_pairs={{0,1},{1,0},{2,3},{3,2},{4,5},{5,4},{6,7},{7,6},{8,9},{9,8},{10,11... | collective-permute-start | bytes 1179656 | tf_op jit(solution)/shard_map/ppermute | solution.py:55
  41.2 4.5 %collective-permute-start.12 = (bf16[256,768]{1,0:T(8,128)(2,1)S(1)}, bf16[256,768]{1,0:T(8,128)(2,1)S(1)}, u32[]{:S(2)}, u32[]{:S(2)}) collective-permute-start(bf16[256,768]{1,0:T(8,128)(2,1)S(1)} %collective-permute-done.8.refs_1_), channel_id=1, source_target_pairs={{0,1},{1,0},{2,3},{3,2},{4,5},{5,4},{6,7},{7,6},{8,9},{9,8},{10,11... | collective-permute-start | bytes 1179656 | tf_op jit(solution)/shard_map/ppermute | solution.py:55
  52.1 4.8 %collective-permute-start.13 = (f16[264,768]{1,0:T(8,128)(2,1)S(1)}, f16[264,768]{1,0:T(8,128)(2,1)S(1)}, u32[]{:S(2)}, u32[]{:S(2)}) collective-permute-start(f16[264,768]{1,0:T(8,128)(2,1)S(1)} %multiply_convert_fusion.6), channel_id=1, source_target_pairs={{0,1},{1,0},{2,3},{3,2},{4,5},{5,4},{6,7},{7,6},{8,9},{9,8},{10,11... | collective-permute-start | bytes 1216520 | tf_op jit(solution)/shard_map/ppermute | solution.py:55
  52.3 4.8 %collective-permute-start.14 = (f16[264,768]{1,0:T(8,128)(2,1)S(1)}, f16[264,768]{1,0:T(8,128)(2,1)S(1)}, u32[]{:S(2)}, u32[]{:S(2)}) collective-permute-start(f16[264,768]{1,0:T(8,128)(2,1)S(1)} %multiply_convert_fusion.5), channel_id=1, source_target_pairs={{0,1},{1,0},{2,3},{3,2},{4,5},{5,4},{6,7},{7,6},{8,9},{9,8},{10,11... | collective-permute-start | bytes 1216520 | tf_op jit(solution)/shard_map/ppermute | solution.py:55
  57.2 20.9 %collective-permute-start.15 = (f16[264,768]{1,0:T(8,128)(2,1)S(1)}, f16[264,768]{1,0:T(8,128)(2,1)S(1)}, u32[]{:S(2)}, u32[]{:S(2)}) collective-permute-start(f16[264,768]{1,0:T(8,128)(2,1)S(1)} %add_convert_fusion.5), channel_id=1, source_target_pairs={{0,12},{1,13},{2,14},{3,15},{4,0},{5,1},{6,2},{7,3},{8,4},{9,5},{1... | collective-permute-start | bytes 1216520 | tf_op jit(solution)/shard_map/ppermute | solution.py:50
  57.2 20.8 %collective-permute-start.16 = (f16[264,768]{1,0:T(8,128)(2,1)S(1)}, f16[264,768]{1,0:T(8,128)(2,1)S(1)}, u32[]{:S(2)}, u32[]{:S(2)}) collective-permute-start(f16[264,768]{1,0:T(8,128)(2,1)S(1)} %add_convert_fusion.4), channel_id=1, source_target_pairs={{0,2},{1,3},{2,0},{3,1},{4,6},{5,7},{6,4},{7,5},{8,10},{9,11},{10,... | collective-permute-start | bytes 1216520 | tf_op jit(solution)/shard_map/ppermute | solution.py:49
  77.4 1.8 %collective-permute-start.17 = (f16[264,768]{1,0:T(8,128)(2,1)S(1)}, f16[264,768]{1,0:T(8,128)(2,1)S(1)}, u32[]{:S(2)}, u32[]{:S(2)}) collective-permute-start(f16[264,768]{1,0:T(8,128)(2,1)S(1)} %multiply_convert_fusion.4), channel_id=1, source_target_pairs={{0,1},{1,0},{2,3},{3,2},{4,5},{5,4},{6,7},{7,6},{8,9},{9,8},{10,11... | collective-permute-start | bytes 1216520 | tf_op jit(solution)/shard_map/ppermute | solution.py:55
  77.5 2.2 %collective-permute-start.18 = (f16[264,768]{1,0:T(8,128)(2,1)S(1)}, f16[264,768]{1,0:T(8,128)(2,1)S(1)}, u32[]{:S(2)}, u32[]{:S(2)}) collective-permute-start(f16[264,768]{1,0:T(8,128)(2,1)S(1)} %multiply_convert_fusion.3), channel_id=1, source_target_pairs={{0,1},{1,0},{2,3},{3,2},{4,5},{5,4},{6,7},{7,6},{8,9},{9,8},{10,11... | collective-permute-start | bytes 1216520 | tf_op jit(solution)/shard_map/ppermute | solution.py:55
  79.8 13.5 %collective-permute-start.19 = (f16[264,768]{1,0:T(8,128)(2,1)S(1)}, f16[264,768]{1,0:T(8,128)(2,1)S(1)}, u32[]{:S(2)}, u32[]{:S(2)}) collective-permute-start(f16[264,768]{1,0:T(8,128)(2,1)S(1)} %add_convert_fusion.3), channel_id=1, source_target_pairs={{0,4},{1,5},{2,6},{3,7},{4,8},{5,9},{6,10},{7,11},{8,12},{9,13},{1... | collective-permute-start | bytes 1216520 | tf_op jit(solution)/shard_map/ppermute | solution.py:50
  80.1 13.2 %collective-permute-start.20 = (f16[264,768]{1,0:T(8,128)(2,1)S(1)}, f16[264,768]{1,0:T(8,128)(2,1)S(1)}, u32[]{:S(2)}, u32[]{:S(2)}) collective-permute-start(f16[264,768]{1,0:T(8,128)(2,1)S(1)} %add_convert_fusion.2), channel_id=1, source_target_pairs={{0,2},{1,3},{2,0},{3,1},{4,6},{5,7},{6,4},{7,5},{8,10},{9,11},{10,... | collective-permute-start | bytes 1216520 | tf_op jit(solution)/shard_map/ppermute | solution.py:49
  84.5 9.0 %collective-permute-start.21 = (f16[264,768]{1,0:T(8,128)(2,1)S(1)}, f16[264,768]{1,0:T(8,128)(2,1)S(1)}, u32[]{:S(2)}, u32[]{:S(2)}) collective-permute-start(f16[264,768]{1,0:T(8,128)(2,1)S(1)} %multiply_convert_fusion.2), channel_id=1, source_target_pairs={{0,1},{1,0},{2,3},{3,2},{4,5},{5,4},{6,7},{7,6},{8,9},{9,8},{10,11... | collective-permute-start | bytes 1216520 | tf_op jit(solution)/shard_map/ppermute | solution.py:55
  84.7 9.0 %collective-permute-start.22 = (f16[264,768]{1,0:T(8,128)(2,1)S(1)}, f16[264,768]{1,0:T(8,128)(2,1)S(1)}, u32[]{:S(2)}, u32[]{:S(2)}) collective-permute-start(f16[264,768]{1,0:T(8,128)(2,1)S(1)} %multiply_convert_fusion.1), channel_id=1, source_target_pairs={{0,1},{1,0},{2,3},{3,2},{4,5},{5,4},{6,7},{7,6},{8,9},{9,8},{10,11... | collective-permute-start | bytes 1216520 | tf_op jit(solution)/shard_map/ppermute | solution.py:55
  93.8 10.6 %collective-permute-start.23 = (f16[264,768]{1,0:T(8,128)(2,1)S(1)}, f16[264,768]{1,0:T(8,128)(2,1)S(1)}, u32[]{:S(2)}, u32[]{:S(2)}) collective-permute-start(f16[264,768]{1,0:T(8,128)(2,1)S(1)} %add_convert_fusion.1), channel_id=1, source_target_pairs={{0,12},{1,13},{2,14},{3,15},{4,0},{5,1},{6,2},{7,3},{8,4},{9,5},{1... | collective-permute-start | bytes 1216520 | tf_op jit(solution)/shard_map/ppermute | solution.py:50
  95.6 10.0 %collective-permute-start.24 = (f16[264,768]{1,0:T(8,128)(2,1)S(1)}, f16[264,768]{1,0:T(8,128)(2,1)S(1)}, u32[]{:S(2)}, u32[]{:S(2)}) collective-permute-start(f16[264,768]{1,0:T(8,128)(2,1)S(1)} %add_convert_fusion), channel_id=1, source_target_pairs={{0,2},{1,3},{2,0},{3,1},{4,6},{5,7},{6,4},{7,5},{8,10},{9,11},{10,... | collective-permute-start | bytes 1216520 | tf_op jit(solution)/shard_map/ppermute | solution.py:49
  101.4 4.5 %collective-permute-start.25 = (f16[264,768]{1,0:T(8,128)(2,1)S(1)}, f16[264,768]{1,0:T(8,128)(2,1)S(1)}, u32[]{:S(2)}, u32[]{:S(2)}) collective-permute-start(f16[264,768]{1,0:T(8,128)(2,1)S(1)} %multiply_convert_fusion), channel_id=1, source_target_pairs={{0,1},{1,0},{2,3},{3,2},{4,5},{5,4},{6,7},{7,6},{8,9},{9,8},{10,11... | collective-permute-start | bytes 1216520 | tf_op jit(solution)/shard_map/ppermute | solution.py:55
  105.8 1.0 copy-start.1
where the time goes:
time: 108 us
  Pallas kernels  53.3 us (49%)
  starting transfers between devices  24 us (22%)
  waiting for transfers between devices  23.1 us (21%)
  other arithmetic  3.94 us (4%)
  local copies, waits for them, and re-layouts  2.47 us (2%)
    pallas_call x4, Pallas kernels, score_group(): pl.pallas_call(functools.partial(score_kernel, slots, fetch), out_shape=o...  24 us
    pallas_call x4, Pallas kernels, sum_group(): pl.pallas_call(functools.partial(sum_kernel, slots, sources), out_shape=(...  22.5 us
    ppermute x6, waiting for transfers between devices, moved(): lax.ppermute(value, 'blk', [(i, (i + shift) % count) for i in range(count)])  18.3 us
    ppermute x6, starting transfers between devices, moved(): return lax.ppermute(value, 'blk', [(i, i ^ 2) for i in range(count)])  13.5 us
    pallas_call x1, Pallas kernels, middle_group(): pl.pallas_call(functools.partial(middle_kernel, slots, sizes.listed, earl...  6.3 us
    ppermute x6, starting transfers between devices, moved(): lax.ppermute(value, 'blk', [(i, (i + shift) % count) for i in range(count)])  5.73 us
    ppermute x14, starting transfers between devices, other_core(): return lax.ppermute(value, 'blk', [(i, i ^ 1) for i in range(count)])  4.78 us
    ppermute x6, waiting for transfers between devices, moved(): return lax.ppermute(value, 'blk', [(i, i ^ 2) for i in range(count)])  2.58 us
  transfers between devices with their start and end apart: 26, of which 11 were waited for; matrix products, arithmetic and copies ran while one was open for 3% of the time, Pallas kernels for 44%

commit v1 on v0

--- a/solution.py
+++ b/solution.py
@@ -284,15 +284,30 @@
     store_totals(out_refs, totals)
 
 
-def middle_kernel(slots, listed, earlier, order_ref, counts_ref, x, *refs):
+def middle_kernel(
+    slots, near_slots, sources, listed, earlier, order_ref, counts_ref, x, near_tiles_ref, *refs
+):
     pieces = len(slots)
+    both = slots + near_slots
     stat_refs = refs[: 2 * earlier]
     piece_refs = refs[2 * earlier : 2 * earlier + pieces]
     refs = refs[2 * earlier + pieces :]
     logs_ref, shares = refs[:2]
-    out_refs = refs[2 : 2 + pieces]
-    panels, norms, tiles, tops, masses, totals = refs[2 + pieces :]
+    out_refs = refs[2 : 2 + len(both)]
+    panels, norms, tiles, tops, masses, totals, tile_sem = refs[2 + len(both) :]
     blocks = x.shape[0] // BLOCK
+
+    def incoming(k, i):
+        source = near_tiles_ref.at[sources[k] + i]
+        return pltpu.make_async_copy(
+            source, tiles.at[(pieces + k) * blocks + i], tile_sem.at[k * blocks + i]
+        )
+
+    def ready(p, i):
+        if p >= pieces:
+            incoming(p - pieces, i).wait()
+
+    over_tiles(near_slots, counts_ref, lambda k, i: incoming(k, i).start())
     clear_sums(out_refs, totals)
     find_norms(piece_refs, panels, norms)
     score_loop(
@@ -309,7 +324,7 @@
     whole = jnp.sum(factor * mass, axis=0)
     logs_ref[...] = (highest + jnp.log2(whole)) * (1.0 / LOG2E)
     shares[...] = (factor / whole[None]).reshape(listed * blocks, width)
-    sum_loop(slots, order_ref, counts_ref, x, shares, out_refs, totals, tiles, lambda p, i: None)
+    sum_loop(both, order_ref, counts_ref, x, shares, out_refs, totals, tiles, ready)
     store_totals(out_refs, totals)
 
 
@@ -393,27 +408,32 @@
     )(order, counts, rows, shares, *[tiles[which] for which in used])
 
 
-def middle_group(sizes, slots, order, counts, rows, tops, masses, pieces):
+def middle_group(
+    sizes, slots, near_slots, order, counts, rows, tops, masses, pieces, places, tiles
+):
     count = len(pieces)
+    sums = len(slots) + len(near_slots)
     earlier = len(tops)
+    sources = [places[slot][1] for slot in near_slots]
     return pl.pallas_call(
-        functools.partial(middle_kernel, slots, sizes.listed, earlier),
+        functools.partial(middle_kernel, slots, near_slots, sources, sizes.listed, earlier),
         out_shape=(jax.ShapeDtypeStruct((sizes.blocks, BLOCK), jnp.float32), sizes.stats)
-        + (sizes.sums,) * count,
-        in_specs=[SMEM, SMEM, VMEM] + [VMEM] * (2 * earlier + count),
-        out_specs=(VMEM, VMEM) + (VMEM,) * count,
+        + (sizes.sums,) * sums,
+        in_specs=[SMEM, SMEM, VMEM, HBM] + [VMEM] * (2 * earlier + count),
+        out_specs=(VMEM, VMEM) + (VMEM,) * sums,
         scratch_shapes=[
             sizes.panels(count),
             sizes.columns(count),
-            sizes.tile_scratch(count),
+            sizes.tile_scratch(sums),
             pltpu.VMEM(sizes.stats.shape, jnp.float32),
             pltpu.VMEM(sizes.stats.shape, jnp.float32),
-            sizes.columns(count),
+            sizes.columns(sums),
+            pltpu.SemaphoreType.DMA((len(near_slots) * sizes.blocks,)),
         ],
         compiler_params=pltpu.CompilerParams(vmem_limit_bytes=VMEM_GRANT),
-        cost_estimate=sizes.cost(slots, 2),
+        cost_estimate=sizes.cost(slots, 3),
         name="middle_group",
-    )(order, counts, rows, *tops, *masses, *pieces)
+    )(order, counts, rows, tiles[places[near_slots[0]][0]], *tops, *masses, *pieces)
 
 
 def add_kernel(mine_ref, back_ref, out_ref):
@@ -477,10 +497,11 @@
     tiles.append(scored[0])
     tops.append(scored[1])
     masses.append(scored[2])
-    log_totals, shares, *far_sums = middle_group(
-        sizes, far_slots, order, counts, rows, tops, masses, [far[q] for q in last]
-    )
-    near_sums = sum_group(sizes, near_slots, order, counts, rows, shares, places, tiles)
+    log_totals, shares, *sums = middle_group(
+        sizes, far_slots, near_slots, order, counts, rows, tops, masses,
+        [far[q] for q in last], places, tiles,
+    )
+    far_sums, near_sums = sums[: len(last)], sums[len(last) :]
     mine = dict(zip(last, near_sums))
     crossed = {q: other_core(packed(v)) for q, v in zip(last, far_sums)}
     total = {q: mine[q] * LINK_SCALE + crossed[q].astype(jnp.float32) for q in last}

time: 108 us -> 109 us (level)
  the two profiles are of different devices: /device:TPU:2 before, /device:TPU:0 now
where the time goes in v1:
time: 109 us; the launch traced here: 108 us
  Pallas kernels  50.8 us (47%)
  waiting for transfers between devices  26.5 us (24%)
  starting transfers between devices  23.3 us (21%)
  other arithmetic  3.99 us (4%)
  local copies, waits for them, and re-layouts  2.47 us (2%)
    pallas_call x4, Pallas kernels, score_group(): pl.pallas_call(functools.partial(score_kernel, slots, fetch), out_shape=o...  25.6 us
    pallas_call x3, Pallas kernels, sum_group(): pl.pallas_call(functools.partial(sum_kernel, slots, sources), out_shape=(...  19.6 us
    ppermute x6, waiting for transfers between devices, moved(): lax.ppermute(value, 'blk', [(i, (i + shift) % count) for i in range(count)])  19.5 us
    ppermute x6, starting transfers between devices, moved(): lax.ppermute(value, 'blk', [(i, (i + shift) % count) for i in range(count)])  12.3 us
    ppermute x14, starting transfers between devices, other_core(): return lax.ppermute(value, 'blk', [(i, i ^ 1) for i in range(count)])  7.44 us
    pallas_call x1, Pallas kernels, middle_group(): pl.pallas_call(functools.partial(middle_kernel, slots, near_slots, source...  5.27 us
    ppermute x14, waiting for transfers between devices, other_core(): return lax.ppermute(value, 'blk', [(i, i ^ 1) for i in range(count)])  4.67 us
    ppermute x6, starting transfers between devices, moved(): return lax.ppermute(value, 'blk', [(i, i ^ 2) for i in range(count)])  3.52 us
  transfers between devices with their start and end apart: 26, of which 12 were waited for; matrix products, arithmetic and copies ran while one was open for 3% of the time, Pallas kernels for 42%

profile of v1, /device:TPU:0, one launch (start us, length us, event | category | flops | bytes accessed | tf_op | source)
XLA Modules:
  0.0 108.1 jit_solution(3582354864434244039)
XLA Ops:
  1.1 2.6 %collective-permute-start.1 = (bf16[256,768]{1,0:T(8,128)(2,1)}, bf16[256,768]{1,0:T(8,128)(2,1)S(1)}, u32[]{:S(2)}, u32[]{:S(2)}) collective-permute-start(bf16[256,768]{1,0:T(8,128)(2,1)} %refs_0_.1), channel_id=1, source_target_pairs={{0,4},{1,5},{2,6},{3,7},{4,8},{5,9},{6,10},{7,11},{8,12},{9,13},{1... | collective-permute-start | bytes 1179656 | tf_op jit(solution)/shard_map/ppermute | solution.py:50
  3.8 1.5 %collective-permute-start = (bf16[256,768]{1,0:T(8,128)(2,1)}, bf16[256,768]{1,0:T(8,128)(2,1)S(1)}, u32[]{:S(2)}, u32[]{:S(2)}) collective-permute-start(bf16[256,768]{1,0:T(8,128)(2,1)} %refs_0_.1), channel_id=1, source_target_pairs={{0,2},{1,3},{2,0},{3,1},{4,6},{5,7},{6,4},{7,5},{8,10},{9,11},{10,... | collective-permute-start | bytes 1179656 | tf_op jit(solution)/shard_map/ppermute | solution.py:49
  5.3 0.7 fusion.9
  6.7 1.0 copy-done
  7.7 6.6 %score_group.4 = (f32[80,256,256]{2,1,0:T(8,128)}, f32[96,256]{1,0:T(8,128)S(1)}, f32[96,256]{1,0:T(8,128)S(1)}, bf16[4096,768]{1,0:T(8,128)(2,1)S(1)}) custom-call(s32[256]{0:T(256)S(1)} %reshape.57.order_ref, s32[16]{0:T(128)S(1)} %convert_reduce_fusion.counts_ref, bf16[4096,768]{1,0:T(8,128)(2,1)} %rows_ref.1, bf16[256,768]{1,0:T(8,128)(2,1)S(1)} %copy-done), custom_call_target="tpu_custom_call" | custom-call | flops 690262592 | bytes 8089014 | tf_op jit(solution)/shard_map/score_group/pallas_call | solution.py:373
  14.3 1.5 %collective-permute-done.1.refs_3_ = bf16[256,768]{1,0:T(8,128)(2,1)S(1)} collective-permute-done((bf16[256,768]{1,0:T(8,128)(2,1)}, bf16[256,768]{1,0:T(8,128)(2,1)S(1)}, u32[]{:S(2)}, u32[]{:S(2)}) %collective-permute-start.1) | collective-permute-done | bytes 393248 | tf_op jit(solution)/shard_map/ppermute | solution.py:50
  16.3 1.7 %collective-permute-start.3 = (bf16[256,768]{1,0:T(8,128)(2,1)S(1)}, bf16[256,768]{1,0:T(8,128)(2,1)S(1)}, u32[]{:S(2)}, u32[]{:S(2)}) collective-permute-start(bf16[256,768]{1,0:T(8,128)(2,1)S(1)} %copy-done), channel_id=1, source_target_pairs={{0,12},{1,13},{2,14},{3,15},{4,0},{5,1},{6,2},{7,3},{8,4},{9,5},{1... | collective-permute-start | bytes 1179656 | tf_op jit(solution)/shard_map/ppermute | solution.py:50
  18.0 1.5 %collective-permute-start.4 = (bf16[256,768]{1,0:T(8,128)(2,1)S(1)}, bf16[256,768]{1,0:T(8,128)(2,1)S(1)}, u32[]{:S(2)}, u32[]{:S(2)}) collective-permute-start(bf16[256,768]{1,0:T(8,128)(2,1)S(1)} %collective-permute-done.1.refs_3_), channel_id=1, source_target_pairs={{0,2},{1,3},{2,0},{3,1},{4,6},{5,7},{6,4},{7,5},{8,10},{9,11},{10,... | collective-permute-start | bytes 1179656 | tf_op jit(solution)/shard_map/ppermute | solution.py:49
  19.5 12.6 %score_group.5 = (f32[80,256,256]{2,1,0:T(8,128)}, f32[96,256]{1,0:T(8,128)S(1)}, f32[96,256]{1,0:T(8,128)S(1)}) custom-call(s32[256]{0:T(256)S(1)} %reshape.57.order_ref, s32[16]{0:T(128)S(1)} %convert_reduce_fusion.counts_ref, bf16[4096,768]{1,0:T(8,128)(2,1)S(1)} %get-tuple-element.68.rows_ref.x, bf16[256,768]{1,0:T(8,128)(2,1)S(1)} %collective-permute-done.2.refs_0_, ...), custom_call_target="tpu_custom_call" | custom-call | flops 3451312896 | bytes 15279250 | tf_op jit(solution)/shard_map/score_group/pallas_call | solution.py:373
  32.8 1.2 %collective-permute-done.10.refs_3_ = bf16[256,768]{1,0:T(8,128)(2,1)S(1)} collective-permute-done((bf16[256,768]{1,0:T(8,128)(2,1)S(1)}, bf16[256,768]{1,0:T(8,128)(2,1)S(1)}, u32[]{:S(2)}, u32[]{:S(2)}) %collective-permute-start.10) | collective-permute-done | bytes 393248 | tf_op jit(solution)/shard_map/ppermute | solution.py:55
  34.0 0.6 collective-permute-done.9.refs_1_
  34.5 1.6 %score_group.6 = (f32[80,256,256]{2,1,0:T(8,128)}, f32[96,256]{1,0:T(8,128)S(1)}, f32[96,256]{1,0:T(8,128)S(1)}) custom-call(s32[256]{0:T(256)S(1)} %reshape.57.order_ref, s32[16]{0:T(128)S(1)} %convert_reduce_fusion.counts_ref, bf16[4096,768]{1,0:T(8,128)(2,1)S(1)} %get-tuple-element.68.rows_ref.x, bf16[256,768]{1,0:T(8,128)(2,1)S(1)} %collective-permute-done.3.refs_0_, ...), custom_call_target="tpu_custom_call" | custom-call | flops 2761050368 | bytes 13481691 | tf_op jit(solution)/shard_map/score_group/pallas_call | solution.py:373
  36.1 9.5 %collective-permute-done.7.refs_0_ = bf16[256,768]{1,0:T(8,128)(2,1)S(1)} collective-permute-done((bf16[256,768]{1,0:T(8,128)(2,1)S(1)}, bf16[256,768]{1,0:T(8,128)(2,1)S(1)}, u32[]{:S(2)}, u32[]{:S(2)}) %collective-permute-start.7) | collective-permute-done | bytes 393248 | tf_op jit(solution)/shard_map/ppermute | solution.py:50
  46.2 4.8 %score_group.7 = (f32[80,256,256]{2,1,0:T(8,128)}, f32[96,256]{1,0:T(8,128)S(1)}, f32[96,256]{1,0:T(8,128)S(1)}) custom-call(s32[256]{0:T(256)S(1)} %reshape.57.order_ref, s32[16]{0:T(128)S(1)} %convert_reduce_fusion.counts_ref, bf16[4096,768]{1,0:T(8,128)(2,1)S(1)} %get-tuple-element.68.rows_ref.x, bf16[256,768]{1,0:T(8,128)(2,1)S(1)} %collective-permute-done.7.refs_0_, ...), custom_call_target="tpu_custom_call" | custom-call | flops 1380525184 | bytes 9886573 | tf_op jit(solution)/shard_map/score_group/pallas_call | solution.py:373
  51.0 5.3 %middle_group.1 = (f32[16,256]{1,0:T(8,128)S(1)}, f32[96,256]{1,0:T(8,128)S(1)}, f32[264,768]{1,0:T(8,128)S(1)}, f32[264,768]{1,0:T(8,128)S(1)}, f32[264,768]{1,0:T(8,128)S(1)}, /*index=5*/f32[264,768]{1,0:T(8,128)S(1)}) custom-call(s32[256]{0:T(256)S(1)} %reshape.57.order_ref, s32[16]{0:T(128)S(1)} %convert_reduce_fusion.counts_ref, ...), custom_call_target="tpu_custom_call" | custom-call | flops 4141575680 | bytes 9886573 | tf_op jit(solution)/shard_map/middle_group/pallas_call | solution.py:418
  56.5 0.6 collective-permute-start.13
  57.1 1.1 %collective-permute-done.14 = f16[264,768]{1,0:T(8,128)(2,1)S(1)} collective-permute-done((f16[264,768]{1,0:T(8,128)(2,1)S(1)}, f16[264,768]{1,0:T(8,128)(2,1)S(1)}, u32[]{:S(2)}, u32[]{:S(2)}) %collective-permute-start.14) | collective-permute-done | bytes 405536 | tf_op jit(solution)/shard_map/ppermute | solution.py:55
  58.9 6.1 %collective-permute-start.15 = (f16[264,768]{1,0:T(8,128)(2,1)S(1)}, f16[264,768]{1,0:T(8,128)(2,1)S(1)}, u32[]{:S(2)}, u32[]{:S(2)}) collective-permute-start(f16[264,768]{1,0:T(8,128)(2,1)S(1)} %add_convert_fusion.5), channel_id=1, source_target_pairs={{0,12},{1,13},{2,14},{3,15},{4,0},{5,1},{6,2},{7,3},{8,4},{9,5},{1... | collective-permute-start | bytes 1216520 | tf_op jit(solution)/shard_map/ppermute | solution.py:50
  65.0 1.9 %sum_group.3 = (f32[264,768]{1,0:T(8,128)S(1)}, f32[264,768]{1,0:T(8,128)S(1)}, f32[264,768]{1,0:T(8,128)S(1)}, f32[264,768]{1,0:T(8,128)S(1)}) custom-call(s32[256]{0:T(256)S(1)} %reshape.57.order_ref, s32[16]{0:T(128)S(1)} %convert_reduce_fusion.counts_ref, bf16[4096,768]{1,0:T(8,128)(2,1)S(1)} %get-tuple-element.68.rows_ref.x, ...), custom_call_target="tpu_custom_call" | custom-call | flops 2761050368 | bytes 13481691 | tf_op jit(solution)/shard_map/sum_group/pallas_call | solution.py:395
  67.0 3.1 %collective-permute-start.18 = (f16[264,768]{1,0:T(8,128)(2,1)S(1)}, f16[264,768]{1,0:T(8,128)(2,1)S(1)}, u32[]{:S(2)}, u32[]{:S(2)}) collective-permute-start(f16[264,768]{1,0:T(8,128)(2,1)S(1)} %multiply_convert_fusion.3), channel_id=1, source_target_pairs={{0,1},{1,0},{2,3},{3,2},{4,5},{5,4},{6,7},{7,6},{8,9},{9,8},{10,11... | collective-permute-start | bytes 1216520 | tf_op jit(solution)/shard_map/ppermute | solution.py:55
  70.3 3.9 %collective-permute-done.15 = f16[264,768]{1,0:T(8,128)(2,1)S(1)} collective-permute-done((f16[264,768]{1,0:T(8,128)(2,1)S(1)}, f16[264,768]{1,0:T(8,128)(2,1)S(1)}, u32[]{:S(2)}, u32[]{:S(2)}) %collective-permute-start.15) | collective-permute-done | bytes 405536 | tf_op jit(solution)/shard_map/ppermute | solution.py:50
  74.1 2.2 %collective-permute-done.16 = f16[264,768]{1,0:T(8,128)(2,1)S(1)} collective-permute-done((f16[264,768]{1,0:T(8,128)(2,1)S(1)}, f16[264,768]{1,0:T(8,128)(2,1)S(1)}, u32[]{:S(2)}, u32[]{:S(2)}) %collective-permute-start.16) | collective-permute-done | bytes 405536 | tf_op jit(solution)/shard_map/ppermute | solution.py:49
  77.0 1.9 %collective-permute-start.19 = (f16[264,768]{1,0:T(8,128)(2,1)S(1)}, f16[264,768]{1,0:T(8,128)(2,1)S(1)}, u32[]{:S(2)}, u32[]{:S(2)}) collective-permute-start(f16[264,768]{1,0:T(8,128)(2,1)S(1)} %add_convert_fusion.3), channel_id=1, source_target_pairs={{0,4},{1,5},{2,6},{3,7},{4,8},{5,9},{6,10},{7,11},{8,12},{9,13},{1... | collective-permute-start | bytes 1216520 | tf_op jit(solution)/shard_map/ppermute | solution.py:50
  78.8 12.9 %sum_group.4 = (f32[264,768]{1,0:T(8,128)S(1)}, f32[264,768]{1,0:T(8,128)S(1)}, f32[264,768]{1,0:T(8,128)S(1)}, f32[264,768]{1,0:T(8,128)S(1)}) custom-call(s32[256]{0:T(256)S(1)} %reshape.57.order_ref, s32[16]{0:T(128)S(1)} %convert_reduce_fusion.counts_ref, bf16[4096,768]{1,0:T(8,128)(2,1)S(1)} %get-tuple-element.68.rows_ref.x, ...), custom_call_target="tpu_custom_call" | custom-call | flops 2761050368 | bytes 13481691 | tf_op jit(solution)/shard_map/sum_group/pallas_call | solution.py:395
  92.0 0.6 collective-permute-start.21
  92.7 0.9 collective-permute-done.22
  94.9 0.6 copy.6
  95.5 4.7 %sum_group.5 = (f32[264,768]{1,0:T(8,128)S(1)}, f32[264,768]{1,0:T(8,128)S(1)}) custom-call(s32[256]{0:T(256)S(1)} %reshape.57.order_ref, s32[16]{0:T(128)S(1)} %convert_reduce_fusion.counts_ref, bf16[4096,768]{1,0:T(8,128)(2,1)S(1)} %get-tuple-element.68.rows_ref.x, f32[96,256]{1,0:T(8,128)S(1)} %get-tuple-element.116.shares, ...), custom_call_target="tpu_custom_call" | custom-call | flops 1380525184 | bytes 9886573 | tf_op jit(solution)/shard_map/sum_group/pallas_call | solution.py:395
  100.3 0.9 collective-permute-start.25
  101.2 4.7 %collective-permute-done.23 = f16[264,768]{1,0:T(8,128)(2,1)S(1)} collective-permute-done((f16[264,768]{1,0:T(8,128)(2,1)S(1)}, f16[264,768]{1,0:T(8,128)(2,1)S(1)}, u32[]{:S(2)}, u32[]{:S(2)}) %collective-permute-start.23) | collective-permute-done | bytes 405536 | tf_op jit(solution)/shard_map/ppermute | solution.py:50
  106.3 0.8 copy-done.1
  107.1 1.0 fusion
  (67 shorter events, 6.6 us)
Async XLA Ops:
  0.6 13.6 %collective-permute-start.2 = (bf16[256,768]{1,0:T(8,128)(2,1)}, bf16[256,768]{1,0:T(8,128)(2,1)S(1)}, u32[]{:S(2)}, u32[]{:S(2)}) collective-permute-start(bf16[256,768]{1,0:T(8,128)(2,1)} %refs_0_.1), channel_id=1, source_target_pairs={{0,1},{1,0},{2,3},{3,2},{4,5},{5,4},{6,7},{7,6},{8,9},{9,8},{10,11... | collective-permute-start | bytes 1179656 | tf_op jit(solution)/shard_map/ppermute | solution.py:55
  1.1 14.6 %collective-permute-start.1 = (bf16[256,768]{1,0:T(8,128)(2,1)}, bf16[256,768]{1,0:T(8,128)(2,1)S(1)}, u32[]{:S(2)}, u32[]{:S(2)}) collective-permute-start(bf16[256,768]{1,0:T(8,128)(2,1)} %refs_0_.1), channel_id=1, source_target_pairs={{0,4},{1,5},{2,6},{3,7},{4,8},{5,9},{6,10},{7,11},{8,12},{9,13},{1... | collective-permute-start | bytes 1179656 | tf_op jit(solution)/shard_map/ppermute | solution.py:50
  3.8 12.0 %collective-permute-start = (bf16[256,768]{1,0:T(8,128)(2,1)}, bf16[256,768]{1,0:T(8,128)(2,1)S(1)}, u32[]{:S(2)}, u32[]{:S(2)}) collective-permute-start(bf16[256,768]{1,0:T(8,128)(2,1)} %refs_0_.1), channel_id=1, source_target_pairs={{0,2},{1,3},{2,0},{3,1},{4,6},{5,7},{6,4},{7,5},{8,10},{9,11},{10,... | collective-permute-start | bytes 1179656 | tf_op jit(solution)/shard_map/ppermute | solution.py:49
  6.7 1.0 copy-start
  15.7 3.8 %collective-permute-start.5 = (bf16[256,768]{1,0:T(8,128)(2,1)S(1)}, bf16[256,768]{1,0:T(8,128)(2,1)S(1)}, u32[]{:S(2)}, u32[]{:S(2)}) collective-permute-start(bf16[256,768]{1,0:T(8,128)(2,1)S(1)} %collective-permute-done.refs_1_), channel_id=1, source_target_pairs={{0,1},{1,0},{2,3},{3,2},{4,5},{5,4},{6,7},{7,6},{8,9},{9,8},{10,11... | collective-permute-start | bytes 1179656 | tf_op jit(solution)/shard_map/ppermute | solution.py:55
  15.7 3.8 %collective-permute-start.6 = (bf16[256,768]{1,0:T(8,128)(2,1)S(1)}, bf16[256,768]{1,0:T(8,128)(2,1)S(1)}, u32[]{:S(2)}, u32[]{:S(2)}) collective-permute-start(bf16[256,768]{1,0:T(8,128)(2,1)S(1)} %collective-permute-done.1.refs_3_), channel_id=1, source_target_pairs={{0,1},{1,0},{2,3},{3,2},{4,5},{5,4},{6,7},{7,6},{8,9},{9,8},{10,11... | collective-permute-start | bytes 1179656 | tf_op jit(solution)/shard_map/ppermute | solution.py:55
  16.3 15.9 %collective-permute-start.3 = (bf16[256,768]{1,0:T(8,128)(2,1)S(1)}, bf16[256,768]{1,0:T(8,128)(2,1)S(1)}, u32[]{:S(2)}, u32[]{:S(2)}) collective-permute-start(bf16[256,768]{1,0:T(8,128)(2,1)S(1)} %copy-done), channel_id=1, source_target_pairs={{0,12},{1,13},{2,14},{3,15},{4,0},{5,1},{6,2},{7,3},{8,4},{9,5},{1... | collective-permute-start | bytes 1179656 | tf_op jit(solution)/shard_map/ppermute | solution.py:50
  18.0 14.2 %collective-permute-start.4 = (bf16[256,768]{1,0:T(8,128)(2,1)S(1)}, bf16[256,768]{1,0:T(8,128)(2,1)S(1)}, u32[]{:S(2)}, u32[]{:S(2)}) collective-permute-start(bf16[256,768]{1,0:T(8,128)(2,1)S(1)} %collective-permute-done.1.refs_3_), channel_id=1, source_target_pairs={{0,2},{1,3},{2,0},{3,1},{4,6},{5,7},{6,4},{7,5},{8,10},{9,11},{10,... | collective-permute-start | bytes 1179656 | tf_op jit(solution)/shard_map/ppermute | solution.py:49
  32.2 1.8 %collective-permute-start.10 = (bf16[256,768]{1,0:T(8,128)(2,1)S(1)}, bf16[256,768]{1,0:T(8,128)(2,1)S(1)}, u32[]{:S(2)}, u32[]{:S(2)}) collective-permute-start(bf16[256,768]{1,0:T(8,128)(2,1)S(1)} %collective-permute-done.4.refs_2_), channel_id=1, source_target_pairs={{0,1},{1,0},{2,3},{3,2},{4,5},{5,4},{6,7},{7,6},{8,9},{9,8},{10,11... | collective-permute-start | bytes 1179656 | tf_op jit(solution)/shard_map/ppermute | solution.py:55
  32.3 2.3 %collective-permute-start.9 = (bf16[256,768]{1,0:T(8,128)(2,1)S(1)}, bf16[256,768]{1,0:T(8,128)(2,1)S(1)}, u32[]{:S(2)}, u32[]{:S(2)}) collective-permute-start(bf16[256,768]{1,0:T(8,128)(2,1)S(1)} %collective-permute-done.3.refs_0_), channel_id=1, source_target_pairs={{0,1},{1,0},{2,3},{3,2},{4,5},{5,4},{6,7},{7,6},{8,9},{9,8},{10,11... | collective-permute-start | bytes 1179656 | tf_op jit(solution)/shard_map/ppermute | solution.py:55
  32.8 12.9 %collective-permute-start.7 = (bf16[256,768]{1,0:T(8,128)(2,1)S(1)}, bf16[256,768]{1,0:T(8,128)(2,1)S(1)}, u32[]{:S(2)}, u32[]{:S(2)}) collective-permute-start(bf16[256,768]{1,0:T(8,128)(2,1)S(1)} %collective-permute-done.4.refs_2_), channel_id=1, source_target_pairs={{0,4},{1,5},{2,6},{3,7},{4,8},{5,9},{6,10},{7,11},{8,12},{9,13},{1... | collective-permute-start | bytes 1179656 | tf_op jit(solution)/shard_map/ppermute | solution.py:50
  32.8 12.9 %collective-permute-start.8 = (bf16[256,768]{1,0:T(8,128)(2,1)S(1)}, bf16[256,768]{1,0:T(8,128)(2,1)S(1)}, u32[]{:S(2)}, u32[]{:S(2)}) collective-permute-start(bf16[256,768]{1,0:T(8,128)(2,1)S(1)} %collective-permute-done.3.refs_0_), channel_id=1, source_target_pairs={{0,2},{1,3},{2,0},{3,1},{4,6},{5,7},{6,4},{7,5},{8,10},{9,11},{10,... | collective-permute-start | bytes 1179656 | tf_op jit(solution)/shard_map/ppermute | solution.py:49
  45.7 5.3 %collective-permute-start.11 = (bf16[256,768]{1,0:T(8,128)(2,1)S(1)}, bf16[256,768]{1,0:T(8,128)(2,1)S(1)}, u32[]{:S(2)}, u32[]{:S(2)}) collective-permute-start(bf16[256,768]{1,0:T(8,128)(2,1)S(1)} %collective-permute-done.7.refs_0_), channel_id=1, source_target_pairs={{0,1},{1,0},{2,3},{3,2},{4,5},{5,4},{6,7},{7,6},{8,9},{9,8},{10,11... | collective-permute-start | bytes 1179656 | tf_op jit(solution)/shard_map/ppermute | solution.py:55
  45.7 5.3 %collective-permute-start.12 = (bf16[256,768]{1,0:T(8,128)(2,1)S(1)}, bf16[256,768]{1,0:T(8,128)(2,1)S(1)}, u32[]{:S(2)}, u32[]{:S(2)}) collective-permute-start(bf16[256,768]{1,0:T(8,128)(2,1)S(1)} %collective-permute-done.8.refs_1_), channel_id=1, source_target_pairs={{0,1},{1,0},{2,3},{3,2},{4,5},{5,4},{6,7},{7,6},{8,9},{9,8},{10,11... | collective-permute-start | bytes 1179656 | tf_op jit(solution)/shard_map/ppermute | solution.py:55
  56.4 1.8 %collective-permute-start.14 = (f16[264,768]{1,0:T(8,128)(2,1)S(1)}, f16[264,768]{1,0:T(8,128)(2,1)S(1)}, u32[]{:S(2)}, u32[]{:S(2)}) collective-permute-start(f16[264,768]{1,0:T(8,128)(2,1)S(1)} %multiply_convert_fusion.5), channel_id=1, source_target_pairs={{0,1},{1,0},{2,3},{3,2},{4,5},{5,4},{6,7},{7,6},{8,9},{9,8},{10,11... | collective-permute-start | bytes 1216520 | tf_op jit(solution)/shard_map/ppermute | solution.py:55
  56.5 2.2 %collective-permute-start.13 = (f16[264,768]{1,0:T(8,128)(2,1)S(1)}, f16[264,768]{1,0:T(8,128)(2,1)S(1)}, u32[]{:S(2)}, u32[]{:S(2)}) collective-permute-start(f16[264,768]{1,0:T(8,128)(2,1)S(1)} %multiply_convert_fusion.6), channel_id=1, source_target_pairs={{0,1},{1,0},{2,3},{3,2},{4,5},{5,4},{6,7},{7,6},{8,9},{9,8},{10,11... | collective-permute-start | bytes 1216520 | tf_op jit(solution)/shard_map/ppermute | solution.py:55
  58.9 15.2 %collective-permute-start.15 = (f16[264,768]{1,0:T(8,128)(2,1)S(1)}, f16[264,768]{1,0:T(8,128)(2,1)S(1)}, u32[]{:S(2)}, u32[]{:S(2)}) collective-permute-start(f16[264,768]{1,0:T(8,128)(2,1)S(1)} %add_convert_fusion.5), channel_id=1, source_target_pairs={{0,12},{1,13},{2,14},{3,15},{4,0},{5,1},{6,2},{7,3},{8,4},{9,5},{1... | collective-permute-start | bytes 1216520 | tf_op jit(solution)/shard_map/ppermute | solution.py:50
  65.0 11.4 %collective-permute-start.16 = (f16[264,768]{1,0:T(8,128)(2,1)S(1)}, f16[264,768]{1,0:T(8,128)(2,1)S(1)}, u32[]{:S(2)}, u32[]{:S(2)}) collective-permute-start(f16[264,768]{1,0:T(8,128)(2,1)S(1)} %add_convert_fusion.4), channel_id=1, source_target_pairs={{0,2},{1,3},{2,0},{3,1},{4,6},{5,7},{6,4},{7,5},{8,10},{9,11},{10,... | collective-permute-start | bytes 1216520 | tf_op jit(solution)/shard_map/ppermute | solution.py:49
  67.0 9.9 %collective-permute-start.18 = (f16[264,768]{1,0:T(8,128)(2,1)S(1)}, f16[264,768]{1,0:T(8,128)(2,1)S(1)}, u32[]{:S(2)}, u32[]{:S(2)}) collective-permute-start(f16[264,768]{1,0:T(8,128)(2,1)S(1)} %multiply_convert_fusion.3), channel_id=1, source_target_pairs={{0,1},{1,0},{2,3},{3,2},{4,5},{5,4},{6,7},{7,6},{8,9},{9,8},{10,11... | collective-permute-start | bytes 1216520 | tf_op jit(solution)/shard_map/ppermute | solution.py:55
  70.2 6.5 %collective-permute-start.17 = (f16[264,768]{1,0:T(8,128)(2,1)S(1)}, f16[264,768]{1,0:T(8,128)(2,1)S(1)}, u32[]{:S(2)}, u32[]{:S(2)}) collective-permute-start(f16[264,768]{1,0:T(8,128)(2,1)S(1)} %multiply_convert_fusion.4), channel_id=1, source_target_pairs={{0,1},{1,0},{2,3},{3,2},{4,5},{5,4},{6,7},{7,6},{8,9},{9,8},{10,11... | collective-permute-start | bytes 1216520 | tf_op jit(solution)/shard_map/ppermute | solution.py:55
  77.0 15.6 %collective-permute-start.19 = (f16[264,768]{1,0:T(8,128)(2,1)S(1)}, f16[264,768]{1,0:T(8,128)(2,1)S(1)}, u32[]{:S(2)}, u32[]{:S(2)}) collective-permute-start(f16[264,768]{1,0:T(8,128)(2,1)S(1)} %add_convert_fusion.3), channel_id=1, source_target_pairs={{0,4},{1,5},{2,6},{3,7},{4,8},{5,9},{6,10},{7,11},{8,12},{9,13},{1... | collective-permute-start | bytes 1216520 | tf_op jit(solution)/shard_map/ppermute | solution.py:50
  78.8 13.7 %collective-permute-start.20 = (f16[264,768]{1,0:T(8,128)(2,1)S(1)}, f16[264,768]{1,0:T(8,128)(2,1)S(1)}, u32[]{:S(2)}, u32[]{:S(2)}) collective-permute-start(f16[264,768]{1,0:T(8,128)(2,1)S(1)} %add_convert_fusion.2), channel_id=1, source_target_pairs={{0,2},{1,3},{2,0},{3,1},{4,6},{5,7},{6,4},{7,5},{8,10},{9,11},{10,... | collective-permute-start | bytes 1216520 | tf_op jit(solution)/shard_map/ppermute | solution.py:49
  91.8 1.8 %collective-permute-start.22 = (f16[264,768]{1,0:T(8,128)(2,1)S(1)}, f16[264,768]{1,0:T(8,128)(2,1)S(1)}, u32[]{:S(2)}, u32[]{:S(2)}) collective-permute-start(f16[264,768]{1,0:T(8,128)(2,1)S(1)} %multiply_convert_fusion.1), channel_id=1, source_target_pairs={{0,1},{1,0},{2,3},{3,2},{4,5},{5,4},{6,7},{7,6},{8,9},{9,8},{10,11... | collective-permute-start | bytes 1216520 | tf_op jit(solution)/shard_map/ppermute | solution.py:55
  92.0 2.2 %collective-permute-start.21 = (f16[264,768]{1,0:T(8,128)(2,1)S(1)}, f16[264,768]{1,0:T(8,128)(2,1)S(1)}, u32[]{:S(2)}, u32[]{:S(2)}) collective-permute-start(f16[264,768]{1,0:T(8,128)(2,1)S(1)} %multiply_convert_fusion.2), channel_id=1, source_target_pairs={{0,1},{1,0},{2,3},{3,2},{4,5},{5,4},{6,7},{7,6},{8,9},{9,8},{10,11... | collective-permute-start | bytes 1216520 | tf_op jit(solution)/shard_map/ppermute | solution.py:55
  94.3 11.5 %collective-permute-start.23 = (f16[264,768]{1,0:T(8,128)(2,1)S(1)}, f16[264,768]{1,0:T(8,128)(2,1)S(1)}, u32[]{:S(2)}, u32[]{:S(2)}) collective-permute-start(f16[264,768]{1,0:T(8,128)(2,1)S(1)} %add_convert_fusion.1), channel_id=1, source_target_pairs={{0,12},{1,13},{2,14},{3,15},{4,0},{5,1},{6,2},{7,3},{8,4},{9,5},{1... | collective-permute-start | bytes 1216520 | tf_op jit(solution)/shard_map/ppermute | solution.py:50
  94.4 11.5 %collective-permute-start.24 = (f16[264,768]{1,0:T(8,128)(2,1)S(1)}, f16[264,768]{1,0:T(8,128)(2,1)S(1)}, u32[]{:S(2)}, u32[]{:S(2)}) collective-permute-start(f16[264,768]{1,0:T(8,128)(2,1)S(1)} %add_convert_fusion), channel_id=1, source_target_pairs={{0,2},{1,3},{2,0},{3,1},{4,6},{5,7},{6,4},{7,5},{8,10},{9,11},{10,... | collective-permute-start | bytes 1216520 | tf_op jit(solution)/shard_map/ppermute | solution.py:49
  100.3 5.9 %collective-permute-start.25 = (f16[264,768]{1,0:T(8,128)(2,1)S(1)}, f16[264,768]{1,0:T(8,128)(2,1)S(1)}, u32[]{:S(2)}, u32[]{:S(2)}) collective-permute-start(f16[264,768]{1,0:T(8,128)(2,1)S(1)} %multiply_convert_fusion), channel_id=1, source_target_pairs={{0,1},{1,0},{2,3},{3,2},{4,5},{5,4},{6,7},{7,6},{8,9},{9,8},{10,11... | collective-permute-start | bytes 1216520 | tf_op jit(solution)/shard_map/ppermute | solution.py:55
  106.1 1.0 copy-start.1

commit v2 on v0

--- a/solution.py
+++ b/solution.py
@@ -262,9 +262,13 @@
     over_tiles(slots, counts_ref, lambda p, i: outgoing(p * blocks + i).wait())
 
 
-def sum_kernel(slots, sources, order_ref, counts_ref, x, shares, *refs):
+def sum_kernel(slots, sources, with_prior, order_ref, counts_ref, x, shares, *refs):
     pieces = len(slots)
     arrays = len({which for which, _ in sources})
+    if with_prior:
+        prior_ref, *refs, prior, prior_sem = refs
+        bring = pltpu.make_async_copy(prior_ref, prior, prior_sem)
+        bring.start()
     tiles_refs, refs = refs[:arrays], refs[arrays:]
     out_refs = refs[:pieces]
     blocks = x.shape[0] // BLOCK
@@ -277,6 +281,9 @@
 
     over_tiles(slots, counts_ref, lambda p, i: incoming(p, i).start())
     clear_sums(out_refs, totals)
+    if with_prior:
+        bring.wait()
+        out_refs[0][pl.ds(0, prior.shape[0])] = PRIOR_MASS * prior[...].astype(jnp.float32)
     sum_loop(
         slots, order_ref, counts_ref, x, shares, out_refs, totals, tiles,
         lambda p, i: incoming(p, i).wait(),
@@ -373,24 +380,25 @@
     )(order, counts, rows, *pieces)
 
 
-def sum_group(sizes, slots, order, counts, rows, shares, places, tiles):
+def sum_group(sizes, slots, order, counts, rows, shares, places, tiles, prior):
     count = len(slots)
     used = sorted({places[slot][0] for slot in slots})
     sources = [(used.index(places[slot][0]), places[slot][1]) for slot in slots]
     return pl.pallas_call(
-        functools.partial(sum_kernel, slots, sources),
+        functools.partial(sum_kernel, slots, sources, bool(prior)),
         out_shape=(sizes.sums,) * count,
-        in_specs=[SMEM, SMEM, VMEM, VMEM] + [HBM] * len(used),
+        in_specs=[SMEM, SMEM, VMEM, VMEM] + [HBM] * (len(prior) + len(used)),
         out_specs=(VMEM,) * count,
         scratch_shapes=[
             sizes.columns(count),
             sizes.tile_scratch(count),
             pltpu.SemaphoreType.DMA((count * sizes.blocks,)),
-        ],
+        ]
+        + [pltpu.VMEM((sizes.cent, sizes.width), jnp.bfloat16), pltpu.SemaphoreType.DMA] * len(prior),
         compiler_params=pltpu.CompilerParams(vmem_limit_bytes=VMEM_GRANT),
         cost_estimate=sizes.cost(slots, 1),
         name="sum_group",
-    )(order, counts, rows, shares, *[tiles[which] for which in used])
+    )(order, counts, rows, shares, *prior, *[tiles[which] for which in used])
 
 
 def middle_group(sizes, slots, order, counts, rows, tops, masses, pieces):
@@ -480,7 +488,7 @@
     log_totals, shares, *far_sums = middle_group(
         sizes, far_slots, order, counts, rows, tops, masses, [far[q] for q in last]
     )
-    near_sums = sum_group(sizes, near_slots, order, counts, rows, shares, places, tiles)
+    near_sums = sum_group(sizes, near_slots, order, counts, rows, shares, places, tiles, ())
     mine = dict(zip(last, near_sums))
     crossed = {q: other_core(packed(v)) for q, v in zip(last, far_sums)}
     total = {q: mine[q] * LINK_SCALE + crossed[q].astype(jnp.float32) for q in last}
@@ -494,7 +502,10 @@
             moved(value, shift if shift is None else -shift)
             for value, (_, _, shift) in zip(leaving, stage)
         ]
-        sums = sum_group(sizes, local_slots(members), order, counts, rows, shares, places, tiles)
+        prior = (centroids,) if members == groups[0] else ()
+        sums = sum_group(
+            sizes, local_slots(members), order, counts, rows, shares, places, tiles, prior
+        )
         crossed = {q: other_core(packed(v)) for q, v in zip(members, sums[1::2])}
         arriving = lax.optimization_barrier(arriving)
         for value, (_, source, _) in zip(arriving, stage):
@@ -506,9 +517,7 @@
                 part = near_sum * LINK_SCALE
             total[q] = part + crossed[q].astype(jnp.float32)
     own_sums = total[own] * (1.0 / LINK_SCALE)
-    updated = (own_sums[:cent] + PRIOR_MASS * centroids.astype(jnp.float32)) / (
-        own_sums[cent, :cent][:, None] + PRIOR_MASS
-    )
+    updated = own_sums[:cent] / (own_sums[cent, :cent][:, None] + PRIOR_MASS)
     return updated, log_totals.reshape(-1)
 
 

time: 108 us -> 108 us (level)
  the two profiles are of different devices: /device:TPU:2 before, /device:TPU:0 now
where the time goes in v2:
time: 108 us; the launch traced here: 106 us
  Pallas kernels  53.5 us (50%)
  starting transfers between devices  26 us (24%)
  waiting for transfers between devices  20.1 us (19%)
  other arithmetic  3.96 us (4%)
  local copies, waits for them, and re-layouts  1.69 us (2%)
    pallas_call x4, Pallas kernels, score_group(): pl.pallas_call(functools.partial(score_kernel, slots, fetch), out_shape=o...  23.8 us
    pallas_call x4, Pallas kernels, sum_group(): pl.pallas_call(functools.partial(sum_kernel, slots, sources, bool(prior))...  22.9 us
    ppermute x6, starting transfers between devices, moved(): return lax.ppermute(value, 'blk', [(i, i ^ 2) for i in range(count)])  16 us
    ppermute x6, waiting for transfers between devices, moved(): lax.ppermute(value, 'blk', [(i, (i + shift) % count) for i in range(count)])  15.1 us
    ppermute x6, starting transfers between devices, moved(): lax.ppermute(value, 'blk', [(i, (i + shift) % count) for i in range(count)])  6.44 us
    pallas_call x1, Pallas kernels, middle_group(): pl.pallas_call(functools.partial(middle_kernel, slots, sizes.listed, earl...  6.3 us
    ppermute x14, starting transfers between devices, other_core(): return lax.ppermute(value, 'blk', [(i, i ^ 1) for i in range(count)])  3.55 us
    ppermute x6, waiting for transfers between devices, moved(): return lax.ppermute(value, 'blk', [(i, i ^ 2) for i in range(count)])  3.53 us
  transfers between devices with their start and end apart: 26, of which 9 were waited for; matrix products, arithmetic and copies ran while one was open for 3% of the time, Pallas kernels for 44%

profile of v2, /device:TPU:0, one launch (start us, length us, event | category | flops | bytes accessed | tf_op | source)
XLA Modules:
  0.0 106.2 jit_solution(17238917632215639002)
XLA Ops:
  0.6 3.0 %collective-permute-start = (bf16[256,768]{1,0:T(8,128)(2,1)}, bf16[256,768]{1,0:T(8,128)(2,1)S(1)}, u32[]{:S(2)}, u32[]{:S(2)}) collective-permute-start(bf16[256,768]{1,0:T(8,128)(2,1)} %refs_0_.3), channel_id=1, source_target_pairs={{0,2},{1,3},{2,0},{3,1},{4,6},{5,7},{6,4},{7,5},{8,10},{9,11},{10,... | collective-permute-start | bytes 1179656 | tf_op jit(solution)/shard_map/ppermute | solution.py:49
  3.7 1.6 %collective-permute-start.1 = (bf16[256,768]{1,0:T(8,128)(2,1)}, bf16[256,768]{1,0:T(8,128)(2,1)S(1)}, u32[]{:S(2)}, u32[]{:S(2)}) collective-permute-start(bf16[256,768]{1,0:T(8,128)(2,1)} %refs_0_.3), channel_id=1, source_target_pairs={{0,4},{1,5},{2,6},{3,7},{4,8},{5,9},{6,10},{7,11},{8,12},{9,13},{1... | collective-permute-start | bytes 1179656 | tf_op jit(solution)/shard_map/ppermute | solution.py:50
  5.2 0.7 fusion.8
  6.6 1.0 copy-done
  7.6 6.6 %score_group.4 = (f32[80,256,256]{2,1,0:T(8,128)}, f32[96,256]{1,0:T(8,128)S(1)}, f32[96,256]{1,0:T(8,128)S(1)}, bf16[4096,768]{1,0:T(8,128)(2,1)S(1)}) custom-call(s32[256]{0:T(256)S(1)} %reshape.57.order_ref, s32[16]{0:T(128)S(1)} %convert_reduce_fusion.counts_ref, bf16[4096,768]{1,0:T(8,128)(2,1)} %rows_ref.1, bf16[256,768]{1,0:T(8,128)(2,1)S(1)} %copy-done), custom_call_target="tpu_custom_call" | custom-call | flops 690262592 | bytes 8089014 | tf_op jit(solution)/shard_map/score_group/pallas_call | solution.py:365
  14.2 2.2 %collective-permute-done.1.refs_3_ = bf16[256,768]{1,0:T(8,128)(2,1)S(1)} collective-permute-done((bf16[256,768]{1,0:T(8,128)(2,1)}, bf16[256,768]{1,0:T(8,128)(2,1)S(1)}, u32[]{:S(2)}, u32[]{:S(2)}) %collective-permute-start.1) | collective-permute-done | bytes 393248 | tf_op jit(solution)/shard_map/ppermute | solution.py:50
  16.9 1.7 %collective-permute-start.3 = (bf16[256,768]{1,0:T(8,128)(2,1)S(1)}, bf16[256,768]{1,0:T(8,128)(2,1)S(1)}, u32[]{:S(2)}, u32[]{:S(2)}) collective-permute-start(bf16[256,768]{1,0:T(8,128)(2,1)S(1)} %copy-done), channel_id=1, source_target_pairs={{0,12},{1,13},{2,14},{3,15},{4,0},{5,1},{6,2},{7,3},{8,4},{9,5},{1... | collective-permute-start | bytes 1179656 | tf_op jit(solution)/shard_map/ppermute | solution.py:50
  19.1 10.6 %score_group.5 = (f32[80,256,256]{2,1,0:T(8,128)}, f32[96,256]{1,0:T(8,128)S(1)}, f32[96,256]{1,0:T(8,128)S(1)}) custom-call(s32[256]{0:T(256)S(1)} %reshape.57.order_ref, s32[16]{0:T(128)S(1)} %convert_reduce_fusion.counts_ref, bf16[4096,768]{1,0:T(8,128)(2,1)S(1)} %get-tuple-element.68.rows_ref.x, bf16[256,768]{1,0:T(8,128)(2,1)S(1)} %collective-permute-done.2.refs_0_, ...), custom_call_target="tpu_custom_call" | custom-call | flops 3451312896 | bytes 15279250 | tf_op jit(solution)/shard_map/score_group/pallas_call | solution.py:365
  30.6 0.9 collective-permute-done.9.refs_1_
  31.5 0.6 collective-permute-done.10.refs_3_
  32.1 4.2 %score_group.6 = (f32[80,256,256]{2,1,0:T(8,128)}, f32[96,256]{1,0:T(8,128)S(1)}, f32[96,256]{1,0:T(8,128)S(1)}) custom-call(s32[256]{0:T(256)S(1)} %reshape.57.order_ref, s32[16]{0:T(128)S(1)} %convert_reduce_fusion.counts_ref, bf16[4096,768]{1,0:T(8,128)(2,1)S(1)} %get-tuple-element.68.rows_ref.x, bf16[256,768]{1,0:T(8,128)(2,1)S(1)} %collective-permute-done.3.refs_0_, ...), custom_call_target="tpu_custom_call" | custom-call | flops 2761050368 | bytes 13481691 | tf_op jit(solution)/shard_map/score_group/pallas_call | solution.py:365
  36.3 6.9 %collective-permute-done.7.refs_0_ = bf16[256,768]{1,0:T(8,128)(2,1)S(1)} collective-permute-done((bf16[256,768]{1,0:T(8,128)(2,1)S(1)}, bf16[256,768]{1,0:T(8,128)(2,1)S(1)}, u32[]{:S(2)}, u32[]{:S(2)}) %collective-permute-start.7) | collective-permute-done | bytes 393248 | tf_op jit(solution)/shard_map/ppermute | solution.py:50
  43.7 2.4 %score_group.7 = (f32[80,256,256]{2,1,0:T(8,128)}, f32[96,256]{1,0:T(8,128)S(1)}, f32[96,256]{1,0:T(8,128)S(1)}) custom-call(s32[256]{0:T(256)S(1)} %reshape.57.order_ref, s32[16]{0:T(128)S(1)} %convert_reduce_fusion.counts_ref, bf16[4096,768]{1,0:T(8,128)(2,1)S(1)} %get-tuple-element.68.rows_ref.x, bf16[256,768]{1,0:T(8,128)(2,1)S(1)} %collective-permute-done.7.refs_0_, ...), custom_call_target="tpu_custom_call" | custom-call | flops 1380525184 | bytes 9886573 | tf_op jit(solution)/shard_map/score_group/pallas_call | solution.py:365
  46.2 6.3 %middle_group.1 = (f32[16,256]{1,0:T(8,128)S(1)}, f32[96,256]{1,0:T(8,128)S(1)}, f32[264,768]{1,0:T(8,128)S(1)}, f32[264,768]{1,0:T(8,128)S(1)}) custom-call(s32[256]{0:T(256)S(1)} %reshape.57.order_ref, s32[16]{0:T(128)S(1)} %convert_reduce_fusion.counts_ref, bf16[4096,768]{1,0:T(8,128)(2,1)S(1)} %get-tuple-element.68.rows_ref.x, ...), custom_call_target="tpu_custom_call" | custom-call | flops 2761050368 | bytes 9886573 | tf_op jit(solution)/shard_map/middle_group/pallas_call | solution.py:407
  52.7 0.6 collective-permute-start.14
  53.3 2.8 %sum_group.4 = (f32[264,768]{1,0:T(8,128)S(1)}, f32[264,768]{1,0:T(8,128)S(1)}) custom-call(s32[256]{0:T(256)S(1)} %reshape.57.order_ref, s32[16]{0:T(128)S(1)} %convert_reduce_fusion.counts_ref, bf16[4096,768]{1,0:T(8,128)(2,1)S(1)} %get-tuple-element.68.rows_ref.x, f32[96,256]{1,0:T(8,128)S(1)} %get-tuple-element.116.shares, ...), custom_call_target="tpu_custom_call" | custom-call | flops 1380525184 | bytes 9886573 | tf_op jit(solution)/shard_map/sum_group/pallas_call | solution.py:387
  56.6 3.3 %collective-permute-start.16 = (f16[264,768]{1,0:T(8,128)(2,1)S(1)}, f16[264,768]{1,0:T(8,128)(2,1)S(1)}, u32[]{:S(2)}, u32[]{:S(2)}) collective-permute-start(f16[264,768]{1,0:T(8,128)(2,1)S(1)} %add_convert_fusion.4), channel_id=1, source_target_pairs={{0,2},{1,3},{2,0},{3,1},{4,6},{5,7},{6,4},{7,5},{8,10},{9,11},{10,... | collective-permute-start | bytes 1216520 | tf_op jit(solution)/shard_map/ppermute | solution.py:49
  59.9 4.3 %sum_group.5 = (f32[264,768]{1,0:T(8,128)S(1)}, f32[264,768]{1,0:T(8,128)S(1)}, f32[264,768]{1,0:T(8,128)S(1)}, f32[264,768]{1,0:T(8,128)S(1)}) custom-call(s32[256]{0:T(256)S(1)} %reshape.57.order_ref, s32[16]{0:T(128)S(1)} %convert_reduce_fusion.counts_ref, bf16[4096,768]{1,0:T(8,128)(2,1)S(1)} %get-tuple-element.68.rows_ref.x, ...), custom_call_target="tpu_custom_call" | custom-call | flops 2761050368 | bytes 13481691 | tf_op jit(solution)/shard_map/sum_group/pallas_call | solution.py:387
  64.4 0.6 collective-permute-start.18
  65.0 1.6 %collective-permute-done.15 = f16[264,768]{1,0:T(8,128)(2,1)S(1)} collective-permute-done((f16[264,768]{1,0:T(8,128)(2,1)S(1)}, f16[264,768]{1,0:T(8,128)(2,1)S(1)}, u32[]{:S(2)}, u32[]{:S(2)}) %collective-permute-start.15) | collective-permute-done | bytes 405536 | tf_op jit(solution)/shard_map/ppermute | solution.py:50
  66.6 3.0 %collective-permute-done.16 = f16[264,768]{1,0:T(8,128)(2,1)S(1)} collective-permute-done((f16[264,768]{1,0:T(8,128)(2,1)S(1)}, f16[264,768]{1,0:T(8,128)(2,1)S(1)}, u32[]{:S(2)}, u32[]{:S(2)}) %collective-permute-start.16) | collective-permute-done | bytes 405536 | tf_op jit(solution)/shard_map/ppermute | solution.py:49
  70.2 1.0 collective-permute-start.19
  71.3 8.2 %collective-permute-start.20 = (f16[264,768]{1,0:T(8,128)(2,1)S(1)}, f16[264,768]{1,0:T(8,128)(2,1)S(1)}, u32[]{:S(2)}, u32[]{:S(2)}) collective-permute-start(f16[264,768]{1,0:T(8,128)(2,1)S(1)} %add_convert_fusion.2), channel_id=1, source_target_pairs={{0,2},{1,3},{2,0},{3,1},{4,6},{5,7},{6,4},{7,5},{8,10},{9,11},{10,... | collective-permute-start | bytes 1216520 | tf_op jit(solution)/shard_map/ppermute | solution.py:49
  79.5 8.7 %sum_group.6 = (f32[264,768]{1,0:T(8,128)S(1)}, f32[264,768]{1,0:T(8,128)S(1)}, f32[264,768]{1,0:T(8,128)S(1)}, f32[264,768]{1,0:T(8,128)S(1)}) custom-call(s32[256]{0:T(256)S(1)} %reshape.57.order_ref, s32[16]{0:T(128)S(1)} %convert_reduce_fusion.counts_ref, bf16[4096,768]{1,0:T(8,128)(2,1)S(1)} %get-tuple-element.68.rows_ref.x, ...), custom_call_target="tpu_custom_call" | custom-call | flops 2761050368 | bytes 13481691 | tf_op jit(solution)/shard_map/sum_group/pallas_call | solution.py:387
  88.4 0.6 collective-permute-start.22
  89.0 3.1 %collective-permute-done.19 = f16[264,768]{1,0:T(8,128)(2,1)S(1)} collective-permute-done((f16[264,768]{1,0:T(8,128)(2,1)S(1)}, f16[264,768]{1,0:T(8,128)(2,1)S(1)}, u32[]{:S(2)}, u32[]{:S(2)}) %collective-permute-start.19) | collective-permute-done | bytes 405536 | tf_op jit(solution)/shard_map/ppermute | solution.py:50
  92.6 1.9 %collective-permute-start.23 = (f16[264,768]{1,0:T(8,128)(2,1)S(1)}, f16[264,768]{1,0:T(8,128)(2,1)S(1)}, u32[]{:S(2)}, u32[]{:S(2)}) collective-permute-start(f16[264,768]{1,0:T(8,128)(2,1)S(1)} %add_convert_fusion.1), channel_id=1, source_target_pairs={{0,12},{1,13},{2,14},{3,15},{4,0},{5,1},{6,2},{7,3},{8,4},{9,5},{1... | collective-permute-start | bytes 1216520 | tf_op jit(solution)/shard_map/ppermute | solution.py:50
  94.4 0.6 collective-permute-start.24
  95.0 0.6 copy.6
  95.6 7.2 %sum_group.7 = (f32[264,768]{1,0:T(8,128)S(1)}, f32[264,768]{1,0:T(8,128)S(1)}) custom-call(s32[256]{0:T(256)S(1)} %reshape.57.order_ref, s32[16]{0:T(128)S(1)} %convert_reduce_fusion.counts_ref, bf16[4096,768]{1,0:T(8,128)(2,1)S(1)} %get-tuple-element.68.rows_ref.x, f32[96,256]{1,0:T(8,128)S(1)} %get-tuple-element.116.shares, ...), custom_call_target="tpu_custom_call" | custom-call | flops 1380525184 | bytes 9886573 | tf_op jit(solution)/shard_map/sum_group/pallas_call | solution.py:387
  103.0 1.2 %collective-permute-done.23 = f16[264,768]{1,0:T(8,128)(2,1)S(1)} collective-permute-done((f16[264,768]{1,0:T(8,128)(2,1)S(1)}, f16[264,768]{1,0:T(8,128)(2,1)S(1)}, u32[]{:S(2)}, u32[]{:S(2)}) %collective-permute-start.23) | collective-permute-done | bytes 405536 | tf_op jit(solution)/shard_map/ppermute | solution.py:50
  105.2 1.0 slice_divide_fusion
  (68 shorter events, 6.4 us)
Async XLA Ops:
  0.6 13.5 %collective-permute-start = (bf16[256,768]{1,0:T(8,128)(2,1)}, bf16[256,768]{1,0:T(8,128)(2,1)S(1)}, u32[]{:S(2)}, u32[]{:S(2)}) collective-permute-start(bf16[256,768]{1,0:T(8,128)(2,1)} %refs_0_.3), channel_id=1, source_target_pairs={{0,2},{1,3},{2,0},{3,1},{4,6},{5,7},{6,4},{7,5},{8,10},{9,11},{10,... | collective-permute-start | bytes 1179656 | tf_op jit(solution)/shard_map/ppermute | solution.py:49
  3.7 12.7 %collective-permute-start.1 = (bf16[256,768]{1,0:T(8,128)(2,1)}, bf16[256,768]{1,0:T(8,128)(2,1)S(1)}, u32[]{:S(2)}, u32[]{:S(2)}) collective-permute-start(bf16[256,768]{1,0:T(8,128)(2,1)} %refs_0_.3), channel_id=1, source_target_pairs={{0,4},{1,5},{2,6},{3,7},{4,8},{5,9},{6,10},{7,11},{8,12},{9,13},{1... | collective-permute-start | bytes 1179656 | tf_op jit(solution)/shard_map/ppermute | solution.py:50
  5.2 11.1 %collective-permute-start.2 = (bf16[256,768]{1,0:T(8,128)(2,1)}, bf16[256,768]{1,0:T(8,128)(2,1)S(1)}, u32[]{:S(2)}, u32[]{:S(2)}) collective-permute-start(bf16[256,768]{1,0:T(8,128)(2,1)} %refs_0_.3), channel_id=1, source_target_pairs={{0,1},{1,0},{2,3},{3,2},{4,5},{5,4},{6,7},{7,6},{8,9},{9,8},{10,11... | collective-permute-start | bytes 1179656 | tf_op jit(solution)/shard_map/ppermute | solution.py:55
  6.6 1.0 copy-start
  16.3 2.7 %collective-permute-start.5 = (bf16[256,768]{1,0:T(8,128)(2,1)S(1)}, bf16[256,768]{1,0:T(8,128)(2,1)S(1)}, u32[]{:S(2)}, u32[]{:S(2)}) collective-permute-start(bf16[256,768]{1,0:T(8,128)(2,1)S(1)} %collective-permute-done.refs_1_), channel_id=1, source_target_pairs={{0,1},{1,0},{2,3},{3,2},{4,5},{5,4},{6,7},{7,6},{8,9},{9,8},{10,11... | collective-permute-start | bytes 1179656 | tf_op jit(solution)/shard_map/ppermute | solution.py:55
  16.3 2.7 %collective-permute-start.6 = (bf16[256,768]{1,0:T(8,128)(2,1)S(1)}, bf16[256,768]{1,0:T(8,128)(2,1)S(1)}, u32[]{:S(2)}, u32[]{:S(2)}) collective-permute-start(bf16[256,768]{1,0:T(8,128)(2,1)S(1)} %collective-permute-done.1.refs_3_), channel_id=1, source_target_pairs={{0,1},{1,0},{2,3},{3,2},{4,5},{5,4},{6,7},{7,6},{8,9},{9,8},{10,11... | collective-permute-start | bytes 1179656 | tf_op jit(solution)/shard_map/ppermute | solution.py:55
  16.9 12.9 %collective-permute-start.3 = (bf16[256,768]{1,0:T(8,128)(2,1)S(1)}, bf16[256,768]{1,0:T(8,128)(2,1)S(1)}, u32[]{:S(2)}, u32[]{:S(2)}) collective-permute-start(bf16[256,768]{1,0:T(8,128)(2,1)S(1)} %copy-done), channel_id=1, source_target_pairs={{0,12},{1,13},{2,14},{3,15},{4,0},{5,1},{6,2},{7,3},{8,4},{9,5},{1... | collective-permute-start | bytes 1179656 | tf_op jit(solution)/shard_map/ppermute | solution.py:50
  18.6 11.2 %collective-permute-start.4 = (bf16[256,768]{1,0:T(8,128)(2,1)S(1)}, bf16[256,768]{1,0:T(8,128)(2,1)S(1)}, u32[]{:S(2)}, u32[]{:S(2)}) collective-permute-start(bf16[256,768]{1,0:T(8,128)(2,1)S(1)} %collective-permute-done.1.refs_3_), channel_id=1, source_target_pairs={{0,2},{1,3},{2,0},{3,1},{4,6},{5,7},{6,4},{7,5},{8,10},{9,11},{10,... | collective-permute-start | bytes 1179656 | tf_op jit(solution)/shard_map/ppermute | solution.py:49
  29.7 1.8 %collective-permute-start.9 = (bf16[256,768]{1,0:T(8,128)(2,1)S(1)}, bf16[256,768]{1,0:T(8,128)(2,1)S(1)}, u32[]{:S(2)}, u32[]{:S(2)}) collective-permute-start(bf16[256,768]{1,0:T(8,128)(2,1)S(1)} %collective-permute-done.3.refs_0_), channel_id=1, source_target_pairs={{0,1},{1,0},{2,3},{3,2},{4,5},{5,4},{6,7},{7,6},{8,9},{9,8},{10,11... | collective-permute-start | bytes 1179656 | tf_op jit(solution)/shard_map/ppermute | solution.py:55
  29.8 2.3 %collective-permute-start.10 = (bf16[256,768]{1,0:T(8,128)(2,1)S(1)}, bf16[256,768]{1,0:T(8,128)(2,1)S(1)}, u32[]{:S(2)}, u32[]{:S(2)}) collective-permute-start(bf16[256,768]{1,0:T(8,128)(2,1)S(1)} %collective-permute-done.4.refs_2_), channel_id=1, source_target_pairs={{0,1},{1,0},{2,3},{3,2},{4,5},{5,4},{6,7},{7,6},{8,9},{9,8},{10,11... | collective-permute-start | bytes 1179656 | tf_op jit(solution)/shard_map/ppermute | solution.py:55
  30.3 12.9 %collective-permute-start.7 = (bf16[256,768]{1,0:T(8,128)(2,1)S(1)}, bf16[256,768]{1,0:T(8,128)(2,1)S(1)}, u32[]{:S(2)}, u32[]{:S(2)}) collective-permute-start(bf16[256,768]{1,0:T(8,128)(2,1)S(1)} %collective-permute-done.4.refs_2_), channel_id=1, source_target_pairs={{0,4},{1,5},{2,6},{3,7},{4,8},{5,9},{6,10},{7,11},{8,12},{9,13},{1... | collective-permute-start | bytes 1179656 | tf_op jit(solution)/shard_map/ppermute | solution.py:50
  30.3 12.9 %collective-permute-start.8 = (bf16[256,768]{1,0:T(8,128)(2,1)S(1)}, bf16[256,768]{1,0:T(8,128)(2,1)S(1)}, u32[]{:S(2)}, u32[]{:S(2)}) collective-permute-start(bf16[256,768]{1,0:T(8,128)(2,1)S(1)} %collective-permute-done.3.refs_0_), channel_id=1, source_target_pairs={{0,2},{1,3},{2,0},{3,1},{4,6},{5,7},{6,4},{7,5},{8,10},{9,11},{10,... | collective-permute-start | bytes 1179656 | tf_op jit(solution)/shard_map/ppermute | solution.py:49
  43.2 2.9 %collective-permute-start.11 = (bf16[256,768]{1,0:T(8,128)(2,1)S(1)}, bf16[256,768]{1,0:T(8,128)(2,1)S(1)}, u32[]{:S(2)}, u32[]{:S(2)}) collective-permute-start(bf16[256,768]{1,0:T(8,128)(2,1)S(1)} %collective-permute-done.7.refs_0_), channel_id=1, source_target_pairs={{0,1},{1,0},{2,3},{3,2},{4,5},{5,4},{6,7},{7,6},{8,9},{9,8},{10,11... | collective-permute-start | bytes 1179656 | tf_op jit(solution)/shard_map/ppermute | solution.py:55
  43.2 2.9 %collective-permute-start.12 = (bf16[256,768]{1,0:T(8,128)(2,1)S(1)}, bf16[256,768]{1,0:T(8,128)(2,1)S(1)}, u32[]{:S(2)}, u32[]{:S(2)}) collective-permute-start(bf16[256,768]{1,0:T(8,128)(2,1)S(1)} %collective-permute-done.8.refs_1_), channel_id=1, source_target_pairs={{0,1},{1,0},{2,3},{3,2},{4,5},{5,4},{6,7},{7,6},{8,9},{9,8},{10,11... | collective-permute-start | bytes 1179656 | tf_op jit(solution)/shard_map/ppermute | solution.py:55
  52.6 3.5 %collective-permute-start.13 = (f16[264,768]{1,0:T(8,128)(2,1)S(1)}, f16[264,768]{1,0:T(8,128)(2,1)S(1)}, u32[]{:S(2)}, u32[]{:S(2)}) collective-permute-start(f16[264,768]{1,0:T(8,128)(2,1)S(1)} %multiply_convert_fusion.6), channel_id=1, source_target_pairs={{0,1},{1,0},{2,3},{3,2},{4,5},{5,4},{6,7},{7,6},{8,9},{9,8},{10,11... | collective-permute-start | bytes 1216520 | tf_op jit(solution)/shard_map/ppermute | solution.py:55
  52.7 3.5 %collective-permute-start.14 = (f16[264,768]{1,0:T(8,128)(2,1)S(1)}, f16[264,768]{1,0:T(8,128)(2,1)S(1)}, u32[]{:S(2)}, u32[]{:S(2)}) collective-permute-start(f16[264,768]{1,0:T(8,128)(2,1)S(1)} %multiply_convert_fusion.5), channel_id=1, source_target_pairs={{0,1},{1,0},{2,3},{3,2},{4,5},{5,4},{6,7},{7,6},{8,9},{9,8},{10,11... | collective-permute-start | bytes 1216520 | tf_op jit(solution)/shard_map/ppermute | solution.py:55
  56.4 10.2 %collective-permute-start.15 = (f16[264,768]{1,0:T(8,128)(2,1)S(1)}, f16[264,768]{1,0:T(8,128)(2,1)S(1)}, u32[]{:S(2)}, u32[]{:S(2)}) collective-permute-start(f16[264,768]{1,0:T(8,128)(2,1)S(1)} %add_convert_fusion.5), channel_id=1, source_target_pairs={{0,12},{1,13},{2,14},{3,15},{4,0},{5,1},{6,2},{7,3},{8,4},{9,5},{1... | collective-permute-start | bytes 1216520 | tf_op jit(solution)/shard_map/ppermute | solution.py:50
  56.6 13.0 %collective-permute-start.16 = (f16[264,768]{1,0:T(8,128)(2,1)S(1)}, f16[264,768]{1,0:T(8,128)(2,1)S(1)}, u32[]{:S(2)}, u32[]{:S(2)}) collective-permute-start(f16[264,768]{1,0:T(8,128)(2,1)S(1)} %add_convert_fusion.4), channel_id=1, source_target_pairs={{0,2},{1,3},{2,0},{3,1},{4,6},{5,7},{6,4},{7,5},{8,10},{9,11},{10,... | collective-permute-start | bytes 1216520 | tf_op jit(solution)/shard_map/ppermute | solution.py:49
  64.3 5.7 %collective-permute-start.17 = (f16[264,768]{1,0:T(8,128)(2,1)S(1)}, f16[264,768]{1,0:T(8,128)(2,1)S(1)}, u32[]{:S(2)}, u32[]{:S(2)}) collective-permute-start(f16[264,768]{1,0:T(8,128)(2,1)S(1)} %multiply_convert_fusion.4), channel_id=1, source_target_pairs={{0,1},{1,0},{2,3},{3,2},{4,5},{5,4},{6,7},{7,6},{8,9},{9,8},{10,11... | collective-permute-start | bytes 1216520 | tf_op jit(solution)/shard_map/ppermute | solution.py:55
  64.4 5.7 %collective-permute-start.18 = (f16[264,768]{1,0:T(8,128)(2,1)S(1)}, f16[264,768]{1,0:T(8,128)(2,1)S(1)}, u32[]{:S(2)}, u32[]{:S(2)}) collective-permute-start(f16[264,768]{1,0:T(8,128)(2,1)S(1)} %multiply_convert_fusion.3), channel_id=1, source_target_pairs={{0,1},{1,0},{2,3},{3,2},{4,5},{5,4},{6,7},{7,6},{8,9},{9,8},{10,11... | collective-permute-start | bytes 1216520 | tf_op jit(solution)/shard_map/ppermute | solution.py:55
  70.2 21.9 %collective-permute-start.19 = (f16[264,768]{1,0:T(8,128)(2,1)S(1)}, f16[264,768]{1,0:T(8,128)(2,1)S(1)}, u32[]{:S(2)}, u32[]{:S(2)}) collective-permute-start(f16[264,768]{1,0:T(8,128)(2,1)S(1)} %add_convert_fusion.3), channel_id=1, source_target_pairs={{0,4},{1,5},{2,6},{3,7},{4,8},{5,9},{6,10},{7,11},{8,12},{9,13},{1... | collective-permute-start | bytes 1216520 | tf_op jit(solution)/shard_map/ppermute | solution.py:50
  71.3 20.8 %collective-permute-start.20 = (f16[264,768]{1,0:T(8,128)(2,1)S(1)}, f16[264,768]{1,0:T(8,128)(2,1)S(1)}, u32[]{:S(2)}, u32[]{:S(2)}) collective-permute-start(f16[264,768]{1,0:T(8,128)(2,1)S(1)} %add_convert_fusion.2), channel_id=1, source_target_pairs={{0,2},{1,3},{2,0},{3,1},{4,6},{5,7},{6,4},{7,5},{8,10},{9,11},{10,... | collective-permute-start | bytes 1216520 | tf_op jit(solution)/shard_map/ppermute | solution.py:49
  88.2 4.0 %collective-permute-start.21 = (f16[264,768]{1,0:T(8,128)(2,1)S(1)}, f16[264,768]{1,0:T(8,128)(2,1)S(1)}, u32[]{:S(2)}, u32[]{:S(2)}) collective-permute-start(f16[264,768]{1,0:T(8,128)(2,1)S(1)} %multiply_convert_fusion.2), channel_id=1, source_target_pairs={{0,1},{1,0},{2,3},{3,2},{4,5},{5,4},{6,7},{7,6},{8,9},{9,8},{10,11... | collective-permute-start | bytes 1216520 | tf_op jit(solution)/shard_map/ppermute | solution.py:55
  88.4 4.0 %collective-permute-start.22 = (f16[264,768]{1,0:T(8,128)(2,1)S(1)}, f16[264,768]{1,0:T(8,128)(2,1)S(1)}, u32[]{:S(2)}, u32[]{:S(2)}) collective-permute-start(f16[264,768]{1,0:T(8,128)(2,1)S(1)} %multiply_convert_fusion.1), channel_id=1, source_target_pairs={{0,1},{1,0},{2,3},{3,2},{4,5},{5,4},{6,7},{7,6},{8,9},{9,8},{10,11... | collective-permute-start | bytes 1216520 | tf_op jit(solution)/shard_map/ppermute | solution.py:55
  92.1 3.5 %copy-start.1 = (bf16[256,768]{1,0:T(8,128)(2,1)S(1)}, bf16[256,768]{1,0:T(8,128)(2,1)}, u32[]{:S(2)}) copy-start(bf16[256,768]{1,0:T(8,128)(2,1)} %refs_0_.3) | copy-start | bytes 1179652
  92.6 11.6 %collective-permute-start.23 = (f16[264,768]{1,0:T(8,128)(2,1)S(1)}, f16[264,768]{1,0:T(8,128)(2,1)S(1)}, u32[]{:S(2)}, u32[]{:S(2)}) collective-permute-start(f16[264,768]{1,0:T(8,128)(2,1)S(1)} %add_convert_fusion.1), channel_id=1, source_target_pairs={{0,12},{1,13},{2,14},{3,15},{4,0},{5,1},{6,2},{7,3},{8,4},{9,5},{1... | collective-permute-start | bytes 1216520 | tf_op jit(solution)/shard_map/ppermute | solution.py:50
  94.4 10.3 %collective-permute-start.24 = (f16[264,768]{1,0:T(8,128)(2,1)S(1)}, f16[264,768]{1,0:T(8,128)(2,1)S(1)}, u32[]{:S(2)}, u32[]{:S(2)}) collective-permute-start(f16[264,768]{1,0:T(8,128)(2,1)S(1)} %add_convert_fusion), channel_id=1, source_target_pairs={{0,2},{1,3},{2,0},{3,1},{4,6},{5,7},{6,4},{7,5},{8,10},{9,11},{10,... | collective-permute-start | bytes 1216520 | tf_op jit(solution)/shard_map/ppermute | solution.py:49
  102.9 2.1 %collective-permute-start.25 = (f16[264,768]{1,0:T(8,128)(2,1)S(1)}, f16[264,768]{1,0:T(8,128)(2,1)S(1)}, u32[]{:S(2)}, u32[]{:S(2)}) collective-permute-start(f16[264,768]{1,0:T(8,128)(2,1)S(1)} %multiply_convert_fusion), channel_id=1, source_target_pairs={{0,1},{1,0},{2,3},{3,2},{4,5},{5,4},{6,7},{7,6},{8,9},{9,8},{10,11... | collective-permute-start | bytes 1216520 | tf_op jit(solution)/shard_map/ppermute | solution.py:55
